TPU v7x, 512 devices: a whole 4x8x8 slice. The times are simulated.
512 devices in a mesh: seq: 64 (over z, y_hi, core), tensor: 8 (over x, y_lo).
Axes of the slice: x: 4, y: 8 (y_hi: 4, y_lo: 2; y = y_hi * 2 + y_lo), z: 8, core: 2. Of those that a mesh axis runs over, the one named last changes fastest.
Arguments:
- q_in: float32 [16384, 5120], P('seq', 'tensor'), may hold values from -520 to 520
- k_in: float32 [16384, 5120], P('seq', 'tensor'), may hold values from -520 to 520
- v_in: bfloat16 [16384, 5120], P('seq', 'tensor'), may hold values from -12 to 12
- q_gain: float32 [5120], P('tensor'), may hold values from 0.8 to 2
- k_gain: float32 [5120], P('tensor'), may hold values from 0.8 to 2
- frames: int32 [128], replicated, may hold values from 0 to 11, never falling along the last dimension, each value on 1 to 12 neighbouring positions
- adjacent: int32 [128, 128], P('seq'), may hold values 0 or 1
Outputs:
- attended: float32 [16384, 5120], P('seq', 'tensor')
Inputs may be any that keep to these rules, and one draw needn't show every extreme that they name: `frames`: frame numbers never fall from one block to the next, and each frame spans 1 to 12 consecutive blocks.
All inputs are finite; a program needn't handle non-finite values. No bound on the sum of `adjacent` on one device may be relied on, other than what follows from the above.
Results may differ from a plain program's by a relative error of at most 0.012.
The roundings to bfloat16 on the way count: a program that leaves them out, or rounds other values in their place, can miss the bound.
Values may be sent and summed in bfloat16 or wider, within the bound.
A program may use at most 128 MiB of HBM per device.

v0:
```python
import math

import jax
import jax.numpy as jnp
from jax import lax
from jax.sharding import PartitionSpec as P

HEAD_DIM = 128
BLOCK = 128
FRAME_BLK = 12


epsilon = 1e-06
blocked = -1e30


def passed_along(value, axis, steps):
    count = lax.axis_size(axis)
    initial, last = (max(0, -steps), min(count, count - steps))
    return lax.ppermute(value, axis, [(source, source + steps) for source in range(initial, last)])


def normalized(inputs, gain_row, square_sum, full_width):
    return (inputs / jnp.sqrt(square_sum / full_width + epsilon)[:, None] * gain_row).astype(
        jnp.bfloat16
    )


def shards(q_in, k_in, v_in, q_gain, k_gain, frames, adjacent):
    tok_rows = q_in.shape[0]
    width_dev = q_in.shape[1]
    full_width = width_dev * lax.axis_size("tensor")
    q_sum, k_sum = lax.psum((jnp.sum(q_in * q_in, axis=1), jnp.sum(k_in * k_in, axis=1)), "tensor")
    q_norm = normalized(q_in, q_gain, q_sum, full_width)
    k_norm = normalized(k_in, k_gain, k_sum, full_width)
    blk_dev = tok_rows // BLOCK
    reach_span = min((blk_dev + 2 * FRAME_BLK - 2) // blk_dev, lax.axis_size("seq") - 1)
    device = lax.axis_index("seq")
    first_block = device * blk_dev
    query_frames = lax.dynamic_slice_in_dim(frames, first_block, blk_dev, 0)
    score_scale = 1.0 / math.sqrt(HEAD_DIM)
    head_count = width_dev // HEAD_DIM
    own_pair = jnp.stack((k_norm, v_in))
    below_pieces = []
    above_pieces = []
    for distance in range(1, reach_span + 1):
        below_pieces.append(passed_along(own_pair, "seq", distance))
        above_pieces.append(passed_along(own_pair, "seq", -distance))
    pieces = below_pieces[::-1] + [own_pair] + above_pieces
    piece_count = len(pieces)
    window_blocks = piece_count * blk_dev
    margin_blocks = reach_span * blk_dev
    padded_frames = jnp.pad(frames, (margin_blocks, margin_blocks), constant_values=-1000)
    key_frames = lax.dynamic_slice_in_dim(padded_frames, first_block, window_blocks, 0)
    padded_adjacent = jnp.pad(adjacent, ((0, 0), (margin_blocks, margin_blocks)))
    adjacent_rows = lax.dynamic_slice_in_dim(padded_adjacent, first_block, window_blocks, 1)
    frame_gap = jnp.abs(query_frames[:, None] - key_frames[None, :])
    allowed = (frame_gap == 0) | (frame_gap == 1) & (adjacent_rows == 1)

    def piece_scores(q_head, key_head, allowed_piece):
        raw_scores = jnp.dot(q_head, key_head.T, preferred_element_type=jnp.float32) * score_scale
        tiled_scores = raw_scores.reshape(blk_dev, BLOCK, blk_dev, BLOCK)
        tiled_scores = jnp.where(allowed_piece[:, None, :, None], tiled_scores, blocked)
        return tiled_scores.reshape(tok_rows, tok_rows)

    def attend_head(head_index, output):
        column = head_index * HEAD_DIM
        q_head = lax.dynamic_slice_in_dim(q_norm, column, HEAD_DIM, 1)
        key_heads = [lax.dynamic_slice_in_dim(piece[0], column, HEAD_DIM, 1) for piece in pieces]
        values = [lax.dynamic_slice_in_dim(piece[1], column, HEAD_DIM, 1) for piece in pieces]
        piece_allowed = [
            allowed[:, piece_index * blk_dev : (piece_index + 1) * blk_dev]
            for piece_index in range(piece_count)
        ]
        score_parts = []
        for piece_index in range(piece_count):
            key_head = key_heads[piece_index]
            allowed_piece = piece_allowed[piece_index]
            block_scores = piece_scores(q_head, key_head, allowed_piece)
            score_parts.append(block_scores)
        scores = jnp.concatenate(score_parts, axis=1)
        row_max = jnp.max(scores, axis=1, keepdims=True)
        weights = jnp.exp(scores - row_max)
        row_total = jnp.sum(weights, axis=1, keepdims=True)
        rounded_weights = weights.astype(jnp.bfloat16)
        mixed_sum = jnp.zeros((tok_rows, HEAD_DIM), jnp.float32)
        for piece_index in range(piece_count):
            piece_weights = rounded_weights[
                :, piece_index * tok_rows : (piece_index + 1) * tok_rows
            ]
            value_head = values[piece_index]
            term = jnp.dot(piece_weights, value_head, preferred_element_type=jnp.float32)
            mixed_sum = mixed_sum + term
        return lax.dynamic_update_slice_in_dim(output, mixed_sum / row_total, column, 1)

    return lax.fori_loop(0, head_count, attend_head, jnp.zeros((tok_rows, width_dev), jnp.float32))


def solution(mesh):
    return jax.shard_map(
        shards,
        mesh=mesh,
        in_specs=(
            P("seq", "tensor"),
            P("seq", "tensor"),
            P("seq", "tensor"),
            P("tensor"),
            P("tensor"),
            P(),
            P("seq", None),
        ),
        out_specs=P("seq", "tensor"),
        check_vma=False,
    )
```

profile of v0, /device:TPU:266, one launch (start us, length us, event | category | flops | bytes accessed | tf_op | source)
XLA Modules:
  0.0 689.4 jit_solution(4850649797370117515)
XLA Ops:
  1.4 14.3 %all-reduce.2 = (f32[256]{0:T(256)S(1)}, f32[256]{0:T(256)S(1)}) all-reduce(f32[256]{0:T(256)S(1)} %get-tuple-element.687, f32[256]{0:T(256)S(1)} %get-tuple-element.686), channel_id=1, replica_groups=mesh['seq'=64,'tensor'=8] {'tensor'}, use_global_device_ids=true, to_apply=%region_1.0 | all-reduce | flops 512 | bytes 4096 | tf_op jit(solution)/shard_map/psum | solution.py:33
  18.9 8.6 %collective-permute-start = (bf16[2,256,640]{2,1,0:T(8,128)(2,1)}, bf16[2,256,640]{2,1,0:T(8,128)(2,1)S(1)}, u32[]{:S(2)}, u32[]{:S(2)}) collective-permute-start(bf16[2,256,640]{2,1,0:T(8,128)(2,1)} %pad_maximum_fusion), channel_id=1, source_target_pairs={{0,96},{8,104},{16,112},{24,120},{32,128},{40,136},{48,144},{56,15... | collective-permute-start | bytes 1966088 | tf_op jit(solution)/shard_map/ppermute | solution.py:20
  27.6 1.9 collective-permute-start.1
  29.5 2.7 collective-permute-start.10
  32.2 5.5 collective-permute-start.11
  37.7 5.2 collective-permute-start.12
  42.9 31.5 %collective-permute-done = bf16[2,256,640]{2,1,0:T(8,128)(2,1)S(1)} collective-permute-done((bf16[2,256,640]{2,1,0:T(8,128)(2,1)}, bf16[2,256,640]{2,1,0:T(8,128)(2,1)S(1)}, u32[]{:S(2)}, u32[]{:S(2)}) %collective-permute-start) | collective-permute-done | bytes 655392 | tf_op jit(solution)/shard_map/ppermute | solution.py:20
  74.3 1.9 collective-permute-start.13
  76.3 9.4 %collective-permute-done.1 = bf16[2,256,640]{2,1,0:T(8,128)(2,1)S(1)} collective-permute-done((bf16[2,256,640]{2,1,0:T(8,128)(2,1)}, bf16[2,256,640]{2,1,0:T(8,128)(2,1)S(1)}, u32[]{:S(2)}, u32[]{:S(2)}) %collective-permute-start.1) | collective-permute-done | bytes 655392 | tf_op jit(solution)/shard_map/ppermute | solution.py:20
  87.5 77.7 %collective-permute-done.10 = bf16[2,256,640]{2,1,0:T(8,128)(2,1)S(1)} collective-permute-done((bf16[2,256,640]{2,1,0:T(8,128)(2,1)}, bf16[2,256,640]{2,1,0:T(8,128)(2,1)S(1)}, u32[]{:S(2)}, u32[]{:S(2)}) %collective-permute-start.10) | collective-permute-done | bytes 655392 | tf_op jit(solution)/shard_map/ppermute | solution.py:20
  167.4 1.9 collective-permute-start.16
  169.3 8.4 %collective-permute-start.17 = (bf16[2,256,640]{2,1,0:T(8,128)(2,1)}, bf16[2,256,640]{2,1,0:T(8,128)(2,1)}, u32[]{:S(2)}, u32[]{:S(2)}) collective-permute-start(bf16[2,256,640]{2,1,0:T(8,128)(2,1)} %pad_maximum_fusion), channel_id=1, source_target_pairs={{48,0},{56,8},{64,16},{72,24},{80,32},{88,40},{96,48},{104,56},{11... | collective-permute-start | bytes 1966088 | tf_op jit(solution)/shard_map/ppermute | solution.py:20
  177.8 1.9 collective-permute-start.18
  179.7 1.9 collective-permute-start.19
  181.7 12.2 %collective-permute-done.15 = bf16[2,256,640]{2,1,0:T(8,128)(2,1)} collective-permute-done((bf16[2,256,640]{2,1,0:T(8,128)(2,1)}, bf16[2,256,640]{2,1,0:T(8,128)(2,1)}, u32[]{:S(2)}, u32[]{:S(2)}) %collective-permute-start.15) | collective-permute-done | bytes 655392 | tf_op jit(solution)/shard_map/ppermute | solution.py:20
  193.9 68.9 %collective-permute-start.2 = (bf16[2,256,640]{2,1,0:T(8,128)(2,1)}, bf16[2,256,640]{2,1,0:T(8,128)(2,1)}, u32[]{:S(2)}, u32[]{:S(2)}) collective-permute-start(bf16[2,256,640]{2,1,0:T(8,128)(2,1)} %pad_maximum_fusion), channel_id=1, source_target_pairs={{0,80},{8,88},{16,96},{24,104},{32,112},{40,120},{48,128},{56,136}... | collective-permute-start | bytes 1966088 | tf_op jit(solution)/shard_map/ppermute | solution.py:20
  262.8 1.9 collective-permute-start.20
  264.7 11.1 %collective-permute-start.21 = (bf16[2,256,640]{2,1,0:T(8,128)(2,1)}, bf16[2,256,640]{2,1,0:T(8,128)(2,1)}, u32[]{:S(2)}, u32[]{:S(2)}) collective-permute-start(bf16[2,256,640]{2,1,0:T(8,128)(2,1)} %pad_maximum_fusion), channel_id=1, source_target_pairs={{80,0},{88,8},{96,16},{104,24},{112,32},{120,40},{128,48},{136,56}... | collective-permute-start | bytes 1966088 | tf_op jit(solution)/shard_map/ppermute | solution.py:20
  275.8 11.2 %collective-permute-start.22 = (bf16[2,256,640]{2,1,0:T(8,128)(2,1)}, bf16[2,256,640]{2,1,0:T(8,128)(2,1)}, u32[]{:S(2)}, u32[]{:S(2)}) collective-permute-start(bf16[2,256,640]{2,1,0:T(8,128)(2,1)} %pad_maximum_fusion), channel_id=1, source_target_pairs={{88,0},{96,8},{104,16},{112,24},{120,32},{128,40},{136,48},{144,56... | collective-permute-start | bytes 1966088 | tf_op jit(solution)/shard_map/ppermute | solution.py:20
  287.0 3.6 collective-permute-start.23
  290.6 31.2 %collective-permute-done.2 = bf16[2,256,640]{2,1,0:T(8,128)(2,1)} collective-permute-done((bf16[2,256,640]{2,1,0:T(8,128)(2,1)}, bf16[2,256,640]{2,1,0:T(8,128)(2,1)}, u32[]{:S(2)}, u32[]{:S(2)}) %collective-permute-start.2) | collective-permute-done | bytes 655392 | tf_op jit(solution)/shard_map/ppermute | solution.py:20
  323.7 1.9 collective-permute-start.4
  327.1 3.2 collective-permute-done.21
  330.4 38.8 %collective-permute-start.5 = (bf16[2,256,640]{2,1,0:T(8,128)(2,1)}, bf16[2,256,640]{2,1,0:T(8,128)(2,1)S(1)}, u32[]{:S(2)}, u32[]{:S(2)}) collective-permute-start(bf16[2,256,640]{2,1,0:T(8,128)(2,1)} %pad_maximum_fusion), channel_id=1, source_target_pairs={{0,56},{8,64},{16,72},{24,80},{32,88},{40,96},{48,104},{56,112},{6... | collective-permute-start | bytes 1966088 | tf_op jit(solution)/shard_map/ppermute | solution.py:20
  369.2 60.5 %collective-permute-start.6 = (bf16[2,256,640]{2,1,0:T(8,128)(2,1)}, bf16[2,256,640]{2,1,0:T(8,128)(2,1)S(1)}, u32[]{:S(2)}, u32[]{:S(2)}) collective-permute-start(bf16[2,256,640]{2,1,0:T(8,128)(2,1)} %pad_maximum_fusion), channel_id=1, source_target_pairs={{0,48},{8,56},{16,64},{24,72},{32,80},{40,88},{48,96},{56,104},{64... | collective-permute-start | bytes 1966088 | tf_op jit(solution)/shard_map/ppermute | solution.py:20
  429.8 1.9 collective-permute-start.7
  431.7 6.1 collective-permute-start.8
  437.9 1.9 collective-permute-start.9
  443.1 16.7 %collective-permute-done.6 = bf16[2,256,640]{2,1,0:T(8,128)(2,1)S(1)} collective-permute-done((bf16[2,256,640]{2,1,0:T(8,128)(2,1)}, bf16[2,256,640]{2,1,0:T(8,128)(2,1)S(1)}, u32[]{:S(2)}, u32[]{:S(2)}) %collective-permute-start.6) | collective-permute-done | bytes 655392 | tf_op jit(solution)/shard_map/ppermute | solution.py:20
  459.8 27.5 %collective-permute-done.7 = bf16[2,256,640]{2,1,0:T(8,128)(2,1)S(1)} collective-permute-done((bf16[2,256,640]{2,1,0:T(8,128)(2,1)}, bf16[2,256,640]{2,1,0:T(8,128)(2,1)S(1)}, u32[]{:S(2)}, u32[]{:S(2)}) %collective-permute-start.7) | collective-permute-done | bytes 655392 | tf_op jit(solution)/shard_map/ppermute | solution.py:20
  487.3 26.4 %collective-permute-done.8 = bf16[2,256,640]{2,1,0:T(8,128)(2,1)S(1)} collective-permute-done((bf16[2,256,640]{2,1,0:T(8,128)(2,1)}, bf16[2,256,640]{2,1,0:T(8,128)(2,1)S(1)}, u32[]{:S(2)}, u32[]{:S(2)}) %collective-permute-start.8) | collective-permute-done | bytes 655392 | tf_op jit(solution)/shard_map/ppermute | solution.py:20
  516.2 173.2 %while.13 = (s32[]{:T(128)}, f32[256,640]{1,0:T(8,128)}, pred[2,50]{1,0:T(4,128)(4,1)S(1)}, bf16[256,640]{1,0:T(8,128)(2,1)S(1)}, bf16[2,256,640]{2,1,0:T(8,128)...) while((s32[]{:T(128)}, f32[256,640]{1,0:T(8,128)}, ...), condition=%wide.region_31.32_spmd, body=%wide.region_4.31_spmd.sunk | while | flops 849509888 | bytes 85476104 | solution.py:96
  (794 shorter events, 186.2 us)
Async XLA Ops:
  18.9 55.4 %collective-permute-start = (bf16[2,256,640]{2,1,0:T(8,128)(2,1)}, bf16[2,256,640]{2,1,0:T(8,128)(2,1)S(1)}, u32[]{:S(2)}, u32[]{:S(2)}) collective-permute-start(bf16[2,256,640]{2,1,0:T(8,128)(2,1)} %pad_maximum_fusion), channel_id=1, source_target_pairs={{0,96},{8,104},{16,112},{24,120},{32,128},{40,136},{48,144},{56,15... | collective-permute-start | bytes 1966088 | tf_op jit(solution)/shard_map/ppermute | solution.py:20
  27.6 58.1 %collective-permute-start.1 = (bf16[2,256,640]{2,1,0:T(8,128)(2,1)}, bf16[2,256,640]{2,1,0:T(8,128)(2,1)S(1)}, u32[]{:S(2)}, u32[]{:S(2)}) collective-permute-start(bf16[2,256,640]{2,1,0:T(8,128)(2,1)} %pad_maximum_fusion), channel_id=1, source_target_pairs={{0,88},{8,96},{16,104},{24,112},{32,120},{40,128},{48,136},{56,144... | collective-permute-start | bytes 1966088 | tf_op jit(solution)/shard_map/ppermute | solution.py:20
  29.5 135.7 %collective-permute-start.10 = (bf16[2,256,640]{2,1,0:T(8,128)(2,1)}, bf16[2,256,640]{2,1,0:T(8,128)(2,1)S(1)}, u32[]{:S(2)}, u32[]{:S(2)}) collective-permute-start(bf16[2,256,640]{2,1,0:T(8,128)(2,1)} %pad_maximum_fusion), channel_id=1, source_target_pairs={{0,16},{8,24},{16,32},{24,40},{32,48},{40,56},{48,64},{56,72},{64,... | collective-permute-start | bytes 1966088 | tf_op jit(solution)/shard_map/ppermute | solution.py:20
  32.2 135.2 %collective-permute-start.11 = (bf16[2,256,640]{2,1,0:T(8,128)(2,1)}, bf16[2,256,640]{2,1,0:T(8,128)(2,1)S(1)}, u32[]{:S(2)}, u32[]{:S(2)}) collective-permute-start(bf16[2,256,640]{2,1,0:T(8,128)(2,1)} %pad_maximum_fusion), channel_id=1, source_target_pairs={{0,8},{8,16},{16,24},{24,32},{32,40},{40,48},{48,56},{56,64},{64,7... | collective-permute-start | bytes 1966088 | tf_op jit(solution)/shard_map/ppermute | solution.py:20
  37.7 131.7 %collective-permute-start.12 = (bf16[2,256,640]{2,1,0:T(8,128)(2,1)}, bf16[2,256,640]{2,1,0:T(8,128)(2,1)}, u32[]{:S(2)}, u32[]{:S(2)}) collective-permute-start(bf16[2,256,640]{2,1,0:T(8,128)(2,1)} %pad_maximum_fusion), channel_id=1, source_target_pairs={{8,0},{16,8},{24,16},{32,24},{40,32},{48,40},{56,48},{64,56},{72,6... | collective-permute-start | bytes 1966088 | tf_op jit(solution)/shard_map/ppermute | solution.py:20
  74.3 103.5 %collective-permute-start.13 = (bf16[2,256,640]{2,1,0:T(8,128)(2,1)}, bf16[2,256,640]{2,1,0:T(8,128)(2,1)}, u32[]{:S(2)}, u32[]{:S(2)}) collective-permute-start(bf16[2,256,640]{2,1,0:T(8,128)(2,1)} %pad_maximum_fusion), channel_id=1, source_target_pairs={{16,0},{24,8},{32,16},{40,24},{48,32},{56,40},{64,48},{72,56},{80,... | collective-permute-start | bytes 1966088 | tf_op jit(solution)/shard_map/ppermute | solution.py:20
  85.6 94.1 %collective-permute-start.14 = (bf16[2,256,640]{2,1,0:T(8,128)(2,1)}, bf16[2,256,640]{2,1,0:T(8,128)(2,1)}, u32[]{:S(2)}, u32[]{:S(2)}) collective-permute-start(bf16[2,256,640]{2,1,0:T(8,128)(2,1)} %pad_maximum_fusion), channel_id=1, source_target_pairs={{24,0},{32,8},{40,16},{48,24},{56,32},{64,40},{72,48},{80,56},{88,... | collective-permute-start | bytes 1966088 | tf_op jit(solution)/shard_map/ppermute | solution.py:20
  165.2 28.7 %collective-permute-start.15 = (bf16[2,256,640]{2,1,0:T(8,128)(2,1)}, bf16[2,256,640]{2,1,0:T(8,128)(2,1)}, u32[]{:S(2)}, u32[]{:S(2)}) collective-permute-start(bf16[2,256,640]{2,1,0:T(8,128)(2,1)} %pad_maximum_fusion), channel_id=1, source_target_pairs={{32,0},{40,8},{48,16},{56,24},{64,32},{72,40},{80,48},{88,56},{96,... | collective-permute-start | bytes 1966088 | tf_op jit(solution)/shard_map/ppermute | solution.py:20
  167.4 95.4 %collective-permute-start.16 = (bf16[2,256,640]{2,1,0:T(8,128)(2,1)}, bf16[2,256,640]{2,1,0:T(8,128)(2,1)}, u32[]{:S(2)}, u32[]{:S(2)}) collective-permute-start(bf16[2,256,640]{2,1,0:T(8,128)(2,1)} %pad_maximum_fusion), channel_id=1, source_target_pairs={{40,0},{48,8},{56,16},{64,24},{72,32},{80,40},{88,48},{96,56},{104... | collective-permute-start | bytes 1966088 | tf_op jit(solution)/shard_map/ppermute | solution.py:20
  169.3 95.4 %collective-permute-start.17 = (bf16[2,256,640]{2,1,0:T(8,128)(2,1)}, bf16[2,256,640]{2,1,0:T(8,128)(2,1)}, u32[]{:S(2)}, u32[]{:S(2)}) collective-permute-start(bf16[2,256,640]{2,1,0:T(8,128)(2,1)} %pad_maximum_fusion), channel_id=1, source_target_pairs={{48,0},{56,8},{64,16},{72,24},{80,32},{88,40},{96,48},{104,56},{11... | collective-permute-start | bytes 1966088 | tf_op jit(solution)/shard_map/ppermute | solution.py:20
  177.8 98.0 %collective-permute-start.18 = (bf16[2,256,640]{2,1,0:T(8,128)(2,1)}, bf16[2,256,640]{2,1,0:T(8,128)(2,1)}, u32[]{:S(2)}, u32[]{:S(2)}) collective-permute-start(bf16[2,256,640]{2,1,0:T(8,128)(2,1)} %pad_maximum_fusion), channel_id=1, source_target_pairs={{56,0},{64,8},{72,16},{80,24},{88,32},{96,40},{104,48},{112,56},{1... | collective-permute-start | bytes 1966088 | tf_op jit(solution)/shard_map/ppermute | solution.py:20
  179.7 107.2 %collective-permute-start.19 = (bf16[2,256,640]{2,1,0:T(8,128)(2,1)}, bf16[2,256,640]{2,1,0:T(8,128)(2,1)}, u32[]{:S(2)}, u32[]{:S(2)}) collective-permute-start(bf16[2,256,640]{2,1,0:T(8,128)(2,1)} %pad_maximum_fusion), channel_id=1, source_target_pairs={{64,0},{72,8},{80,16},{88,24},{96,32},{104,40},{112,48},{120,56},{... | collective-permute-start | bytes 1966088 | tf_op jit(solution)/shard_map/ppermute | solution.py:20
  193.9 127.9 %collective-permute-start.2 = (bf16[2,256,640]{2,1,0:T(8,128)(2,1)}, bf16[2,256,640]{2,1,0:T(8,128)(2,1)}, u32[]{:S(2)}, u32[]{:S(2)}) collective-permute-start(bf16[2,256,640]{2,1,0:T(8,128)(2,1)} %pad_maximum_fusion), channel_id=1, source_target_pairs={{0,80},{8,88},{16,96},{24,104},{32,112},{40,120},{48,128},{56,136}... | collective-permute-start | bytes 1966088 | tf_op jit(solution)/shard_map/ppermute | solution.py:20
  262.8 60.9 %collective-permute-start.20 = (bf16[2,256,640]{2,1,0:T(8,128)(2,1)}, bf16[2,256,640]{2,1,0:T(8,128)(2,1)}, u32[]{:S(2)}, u32[]{:S(2)}) collective-permute-start(bf16[2,256,640]{2,1,0:T(8,128)(2,1)} %pad_maximum_fusion), channel_id=1, source_target_pairs={{72,0},{80,8},{88,16},{96,24},{104,32},{112,40},{120,48},{128,56},... | collective-permute-start | bytes 1966088 | tf_op jit(solution)/shard_map/ppermute | solution.py:20
  264.7 65.7 %collective-permute-start.21 = (bf16[2,256,640]{2,1,0:T(8,128)(2,1)}, bf16[2,256,640]{2,1,0:T(8,128)(2,1)}, u32[]{:S(2)}, u32[]{:S(2)}) collective-permute-start(bf16[2,256,640]{2,1,0:T(8,128)(2,1)} %pad_maximum_fusion), channel_id=1, source_target_pairs={{80,0},{88,8},{96,16},{104,24},{112,32},{120,40},{128,48},{136,56}... | collective-permute-start | bytes 1966088 | tf_op jit(solution)/shard_map/ppermute | solution.py:20
  275.8 93.4 %collective-permute-start.22 = (bf16[2,256,640]{2,1,0:T(8,128)(2,1)}, bf16[2,256,640]{2,1,0:T(8,128)(2,1)}, u32[]{:S(2)}, u32[]{:S(2)}) collective-permute-start(bf16[2,256,640]{2,1,0:T(8,128)(2,1)} %pad_maximum_fusion), channel_id=1, source_target_pairs={{88,0},{96,8},{104,16},{112,24},{120,32},{128,40},{136,48},{144,56... | collective-permute-start | bytes 1966088 | tf_op jit(solution)/shard_map/ppermute | solution.py:20
  287.0 142.8 %collective-permute-start.23 = (bf16[2,256,640]{2,1,0:T(8,128)(2,1)}, bf16[2,256,640]{2,1,0:T(8,128)(2,1)}, u32[]{:S(2)}, u32[]{:S(2)}) collective-permute-start(bf16[2,256,640]{2,1,0:T(8,128)(2,1)} %pad_maximum_fusion), channel_id=1, source_target_pairs={{96,0},{104,8},{112,16},{120,24},{128,32},{136,40},{144,48},{152,5... | collective-permute-start | bytes 1966088 | tf_op jit(solution)/shard_map/ppermute | solution.py:20
  321.8 109.9 %collective-permute-start.3 = (bf16[2,256,640]{2,1,0:T(8,128)(2,1)}, bf16[2,256,640]{2,1,0:T(8,128)(2,1)}, u32[]{:S(2)}, u32[]{:S(2)}) collective-permute-start(bf16[2,256,640]{2,1,0:T(8,128)(2,1)} %pad_maximum_fusion), channel_id=1, source_target_pairs={{0,72},{8,80},{16,88},{24,96},{32,104},{40,112},{48,120},{56,128},... | collective-permute-start | bytes 1966088 | tf_op jit(solution)/shard_map/ppermute | solution.py:20
  323.7 114.1 %collective-permute-start.4 = (bf16[2,256,640]{2,1,0:T(8,128)(2,1)}, bf16[2,256,640]{2,1,0:T(8,128)(2,1)}, u32[]{:S(2)}, u32[]{:S(2)}) collective-permute-start(bf16[2,256,640]{2,1,0:T(8,128)(2,1)} %pad_maximum_fusion), channel_id=1, source_target_pairs={{0,64},{8,72},{16,80},{24,88},{32,96},{40,104},{48,112},{56,120},{... | collective-permute-start | bytes 1966088 | tf_op jit(solution)/shard_map/ppermute | solution.py:20
  330.4 112.7 %collective-permute-start.5 = (bf16[2,256,640]{2,1,0:T(8,128)(2,1)}, bf16[2,256,640]{2,1,0:T(8,128)(2,1)S(1)}, u32[]{:S(2)}, u32[]{:S(2)}) collective-permute-start(bf16[2,256,640]{2,1,0:T(8,128)(2,1)} %pad_maximum_fusion), channel_id=1, source_target_pairs={{0,56},{8,64},{16,72},{24,80},{32,88},{40,96},{48,104},{56,112},{6... | collective-permute-start | bytes 1966088 | tf_op jit(solution)/shard_map/ppermute | solution.py:20
  369.2 90.5 %collective-permute-start.6 = (bf16[2,256,640]{2,1,0:T(8,128)(2,1)}, bf16[2,256,640]{2,1,0:T(8,128)(2,1)S(1)}, u32[]{:S(2)}, u32[]{:S(2)}) collective-permute-start(bf16[2,256,640]{2,1,0:T(8,128)(2,1)} %pad_maximum_fusion), channel_id=1, source_target_pairs={{0,48},{8,56},{16,64},{24,72},{32,80},{40,88},{48,96},{56,104},{64... | collective-permute-start | bytes 1966088 | tf_op jit(solution)/shard_map/ppermute | solution.py:20
  429.8 57.5 %collective-permute-start.7 = (bf16[2,256,640]{2,1,0:T(8,128)(2,1)}, bf16[2,256,640]{2,1,0:T(8,128)(2,1)S(1)}, u32[]{:S(2)}, u32[]{:S(2)}) collective-permute-start(bf16[2,256,640]{2,1,0:T(8,128)(2,1)} %pad_maximum_fusion), channel_id=1, source_target_pairs={{0,40},{8,48},{16,56},{24,64},{32,72},{40,80},{48,88},{56,96},{64,... | collective-permute-start | bytes 1966088 | tf_op jit(solution)/shard_map/ppermute | solution.py:20
  431.7 82.0 %collective-permute-start.8 = (bf16[2,256,640]{2,1,0:T(8,128)(2,1)}, bf16[2,256,640]{2,1,0:T(8,128)(2,1)S(1)}, u32[]{:S(2)}, u32[]{:S(2)}) collective-permute-start(bf16[2,256,640]{2,1,0:T(8,128)(2,1)} %pad_maximum_fusion), channel_id=1, source_target_pairs={{0,32},{8,40},{16,48},{24,56},{32,64},{40,72},{48,80},{56,88},{64,... | collective-permute-start | bytes 1966088 | tf_op jit(solution)/shard_map/ppermute | solution.py:20
  437.9 77.2 %collective-permute-start.9 = (bf16[2,256,640]{2,1,0:T(8,128)(2,1)}, bf16[2,256,640]{2,1,0:T(8,128)(2,1)S(1)}, u32[]{:S(2)}, u32[]{:S(2)}) collective-permute-start(bf16[2,256,640]{2,1,0:T(8,128)(2,1)} %pad_maximum_fusion), channel_id=1, source_target_pairs={{0,24},{8,32},{16,40},{24,48},{32,56},{40,64},{48,72},{56,80},{64,... | collective-permute-start | bytes 1966088 | tf_op jit(solution)/shard_map/ppermute | solution.py:20
  443.0 73.0 %copy-start = (bf16[2,256,640]{2,1,0:T(8,128)(2,1)}, bf16[2,256,640]{2,1,0:T(8,128)(2,1)S(1)}, u32[]{:S(2)}) copy-start(bf16[2,256,640]{2,1,0:T(8,128)(2,1)S(1)} %collective-permute-done.5) | copy-start | bytes 1966084
  459.8 56.3 %copy-start.2 = (bf16[2,256,640]{2,1,0:T(8,128)(2,1)}, bf16[2,256,640]{2,1,0:T(8,128)(2,1)S(1)}, u32[]{:S(2)}) copy-start(bf16[2,256,640]{2,1,0:T(8,128)(2,1)S(1)} %collective-permute-done.6) | copy-start | bytes 1966084
  487.3 28.7 %copy-start.4 = (bf16[2,256,640]{2,1,0:T(8,128)(2,1)}, bf16[2,256,640]{2,1,0:T(8,128)(2,1)S(1)}, u32[]{:S(2)}) copy-start(bf16[2,256,640]{2,1,0:T(8,128)(2,1)S(1)} %collective-permute-done.7) | copy-start | bytes 1966084
  516.7 6.4 copy-start.3
  516.7 6.4 copy-start.5
  585.9 6.4 copy-start.3
  585.9 6.4 copy-start.5
  620.6 6.4 copy-start.3
  (22 other events, 120.9 us)
where the time goes:
time: 692 us; the launch traced here: 689 us
  starting transfers between devices  254 us (37%)
  waiting for transfers between devices  238 us (34%)
  local copies, waits for them, and re-layouts  100 us (14%)
  matrix products  64.4 us (9%)
  blocking collectives  14.3 us (2%)
  other arithmetic  14.2 us (2%)
    ppermute x24, starting transfers between devices, passed_along(): lax.ppermute(value, axis, [(source, source + steps) for source in range(i...  254 us
    ppermute x24, waiting for transfers between devices, passed_along(): lax.ppermute(value, axis, [(source, source + steps) for source in range(i...  238 us
    slice x60, local copies, waits for them, and re-layouts, attend_head(): piece[1]  57.3 us
    dot_general x125, matrix products, attend_head(): jnp.dot(piece_weights, value_head, preferred_element_type=jnp.float32)  35.7 us
    broadcast_in_dim x250, local copies, waits for them, and re-layouts, piece_scores(): jnp.where(allowed_piece[:, None, :, None], tiled_scores, blocked)  35 us
    dot_general x125, matrix products, piece_scores(): jnp.dot(q_head, key_head.T, preferred_element_type=jnp.float32)  28.7 us
    psum x1, blocking collectives, shards(): lax.psum((jnp.sum(q_in * q_in, axis=1), jnp.sum(k_in * k_in, axis=1)), 't...  14.3 us
  transfers between devices with their start and end apart: 24, of which 11 were waited for; matrix products, arithmetic and copies ran while one was open for 1% of the time, Pallas kernels for 0%

commit v1 on v0

v1 whole, which is shorter than its diff:
```python
import math

import jax
import jax.numpy as jnp
from jax import lax
from jax.experimental import pallas as pl
from jax.experimental.pallas import tpu as pltpu
from jax.sharding import PartitionSpec as P

HD = 128
TOK = 256
HEADS = 5
CHIPS = 4
PLANES = 8
TENSOR = 8
SLOTS = 28
MESH = pl.DeviceIdType.MESH
EPS = 1e-06
BLOCKED = -1e30
EXP2_SCALE = math.log2(math.e) / math.sqrt(HD)


def place():
    s = lax.axis_index("seq")
    return lax.div(s, 8), lax.rem(lax.div(s, 2), 4), lax.rem(s, 2), lax.axis_index("tensor")


def columns(head):
    return pl.ds(pl.multiple_of(head * HD, HD), HD)


def gather_kernel(
    q_ref, k_ref, v_ref, qg_ref, kg_ref, adj_ref,
    kvu, kv4, qu, q4, adju,
    qn, kn, stat, statr, relay,
    ssem, lsem, ru, r4, rq, ra, rrelay, rstat,
):
    z, h, k, t = place()
    other = 1 - k

    def dev(zz, hh, kk):
        return (lax.rem(zz + PLANES, PLANES) * 8 + hh * 2 + kk, t)

    def chip(step):
        return lax.rem(h + step, CHIPS)

    sends = []
    locals_ = []

    def send(src, dst, rsem, device):
        copy = pltpu.make_async_remote_copy(
            src_ref=src, dst_ref=dst, send_sem=ssem.at[len(sends)], recv_sem=rsem,
            device_id=device, device_id_type=MESH,
        )
        sends.append(copy)
        copy.start()
        return copy

    def local(src, dst):
        copy = pltpu.make_async_copy(src, dst, lsem.at[len(locals_)])
        locals_.append(copy)
        copy.start()

    def arrived(dst, rsem):
        pltpu.make_async_copy(dst, dst, rsem).wait()

    barrier = pltpu.get_barrier_semaphore()
    peers = [dev(z, h, other)]
    for step in (1, 2, 3):
        peers += [dev(z, chip(step), 0), dev(z, chip(step), 1)]
    for zz in (z + 1, z - 1):
        peers += [dev(zz, h, 0), dev(zz, h, 1)]
    s_me = lax.axis_index("seq")
    for step in range(1, TENSOR):
        peers.append((s_me, lax.rem(t + step, TENSOR)))
    for peer in peers:
        pl.semaphore_signal(barrier, inc=1, device_id=peer, device_id_type=MESH)

    eye = lax.broadcasted_iota(jnp.int32, (128, 128), 0) == lax.broadcasted_iota(
        jnp.int32, (128, 128), 1
    )
    rows = []
    for ref in (q_ref, k_ref):
        for half in range(2):
            part = ref[half * 128 : (half + 1) * 128, :]
            column = jnp.sum(part * part, axis=1, keepdims=True)
            rows.append(jnp.sum(jnp.where(eye, column, 0.0), axis=0, keepdims=True))
    mine = jnp.concatenate(rows + [jnp.zeros((4, 128), jnp.float32)], axis=0)
    stat[...] = mine
    statr[t] = mine

    pl.semaphore_wait(barrier, len(peers))

    for step in range(1, TENSOR):
        send(stat, statr.at[t], rstat.at[t], (s_me, lax.rem(t + step, TENSOR)))

    def u_slot(position, core):
        return position + 12 - 4 * core

    def spread_u(v, hp, src):
        p = 2 * hp + k
        slot = u_slot(p, other)
        send(src, kvu.at[v, u_slot(p - 8, k)], ru.at[v, u_slot(p - 8, k)], dev(z + 1, h, k))
        send(src, kvu.at[v, u_slot(p + 8, k)], ru.at[v, u_slot(p + 8, k)], dev(z - 1, h, k))
        send(src, kvu.at[v, slot], ru.at[v, slot], dev(z, h, other))

    def spread_4(v, hp, src):
        slot = 8 + 2 * hp + k
        send(src, kv4.at[v, slot - 8], r4.at[v, slot - 8], dev(z + 1, h, k))
        send(src, kv4.at[v, slot + 8], r4.at[v, slot + 8], dev(z - 1, h, k))
        send(src, kv4.at[v, slot], r4.at[v, slot], dev(z, h, other))

    own = 2 * h + k
    relay_to = {0: (1, 0), 1: (3, 1)}

    def first(v, head):
        side, buf = relay_to[v]
        slot = u_slot(own, k)
        send(head(chip(2)), relay.at[buf], rrelay.at[buf], dev(z, chip(side), k))
        for step in (1, 3):
            send(head(chip(step)), kvu.at[v, slot], ru.at[v, slot], dev(z, chip(step), k))
        spread_u(v, h, head(h))
        for step in (1, 3):
            send(head(4), kv4.at[v, 8 + own], r4.at[v, 8 + own], dev(z, chip(step), k))
        spread_4(v, h, head(4))
        local(head(h), kvu.at[v, slot])
        local(head(4), kv4.at[v, 8 + own])

    first(0, lambda i: v_ref.at[:, columns(i)])

    for step in range(1, TENSOR):
        j = lax.rem(t + step, TENSOR)
        arrived(statr.at[j], rstat.at[j])
    total = statr[0]
    for j in range(1, TENSOR):
        total = total + statr[j]
    inverse = 1.0 / jnp.sqrt(total / float(HD * HEADS * TENSOR) + EPS)
    for row, (ref, gain, out) in ((2, (k_ref, kg_ref, kn)), (0, (q_ref, qg_ref, qn))):
        for half in range(2):
            lane_row = inverse[row + half : row + half + 1, :]
            column = jnp.sum(jnp.where(eye, lane_row, 0.0), axis=1, keepdims=True)
            for i in range(HEADS):
                part = ref[half * 128 : (half + 1) * 128, i * HD : (i + 1) * HD]
                out[i, half * 128 : (half + 1) * 128, :] = (
                    part * column * gain[:, i * HD : (i + 1) * HD]
                ).astype(jnp.bfloat16)

    first(1, lambda i: kn.at[i])

    core = lax.div(h, 2)
    place_q = 2 * lax.rem(h, 2) + k
    side_q = chip(1 + 2 * k)
    send(qn.at[chip(2)], relay.at[2], rrelay.at[2], dev(z, side_q, k))
    for step in (1, 3):
        send(qn.at[chip(step)], qu.at[place_q], rq.at[place_q], dev(z, chip(step), core))
    for step in (1, 2, 3):
        send(adj_ref, adju.at[place_q], ra.at[place_q], dev(z, chip(step), core))
    to_self = core == k
    own_q = [
        (qn.at[h], qu.at[place_q], rq.at[place_q]),
        (adj_ref, adju.at[place_q], ra.at[place_q]),
    ]
    cross = len(sends)
    for n, (src, dst, sem) in enumerate(own_q):
        @pl.when(to_self)
        def _():
            pltpu.make_async_copy(src, dst, sem).start()

        @pl.when(jnp.logical_not(to_self))
        def _():
            pltpu.make_async_remote_copy(
                src_ref=src, dst_ref=dst, send_sem=ssem.at[150 + n], recv_sem=sem,
                device_id=dev(z, h, other), device_id_type=MESH,
            ).start()
    local(qn.at[4], q4)

    for v in range(2):
        side, buf = relay_to[v]
        back = chip(4 - side)
        arrived(relay.at[buf], rrelay.at[buf])
        slot = u_slot(2 * back + k, k)
        send(relay.at[buf], kvu.at[v, slot], ru.at[v, slot], dev(z, chip(side), k))
        for step in (1, 3):
            hp = chip(step)
            slot = u_slot(2 * hp + k, k)
            arrived(kvu.at[v, slot], ru.at[v, slot])
            spread_u(v, hp, kvu.at[v, slot])
        for step in (4 - side, side):
            hp = chip(step)
            slot = 8 + 2 * hp + k
            arrived(kv4.at[v, slot], r4.at[v, slot])
            if step == 4 - side:
                send(kv4.at[v, slot], kv4.at[v, slot], r4.at[v, slot], dev(z, chip(side), k))
            spread_4(v, hp, kv4.at[v, slot])
        hp = chip(2)
        slot = u_slot(2 * hp + k, k)
        arrived(kvu.at[v, slot], ru.at[v, slot])
        spread_u(v, hp, kvu.at[v, slot])
        slot = 8 + 2 * hp + k
        arrived(kv4.at[v, slot], r4.at[v, slot])
        spread_4(v, hp, kv4.at[v, slot])

    source = chip(3 - 2 * k)
    arrived(relay.at[2], rrelay.at[2])
    where_q = 2 * lax.rem(source, 2) + k
    send(
        relay.at[2], qu.at[where_q], rq.at[where_q],
        dev(z, lax.rem(source + 2, CHIPS), lax.div(source, 2)),
    )

    for step in (0, 1, 3, 2):
        hp = chip(step)
        up = lax.div(hp, 2)
        sign = 1 - 2 * up
        for v in range(2):
            p = 2 * hp + k
            for q in (p - 8, p + 8):
                slot = u_slot(q, k)
                arrived(kvu.at[v, slot], ru.at[v, slot])
                slot_other = u_slot(q, other)
                send(kvu.at[v, slot], kvu.at[v, slot_other], ru.at[v, slot_other], dev(z, h, other))
            target = u_slot(p + 16 * sign, 1 - up)
            send(
                kvu.at[v, u_slot(p + 8 * sign, k)], kvu.at[v, target], ru.at[v, target],
                dev(z - sign, h, 1 - up),
            )
            for slot in (2 * hp + k, 16 + 2 * hp + k):
                arrived(kv4.at[v, slot], r4.at[v, slot])
                send(kv4.at[v, slot], kv4.at[v, slot], r4.at[v, slot], dev(z, h, other))
            if step == 2:
                send(
                    kv4.at[v, 8 + 8 * sign + 2 * hp + k], kv4.at[v, 24 + k], r4.at[v, 24 + k],
                    dev(z - sign, h, k),
                )

    inner = jnp.logical_or(h == 1, h == 2)
    outer = jnp.logical_or(h == 0, h == 3)
    edge = lax.div(h, 2) * 3
    for v in range(2):
        e0, e1 = 24 + k, 26 + k
        arrived(kv4.at[v, e0], r4.at[v, e0])
        send(kv4.at[v, e0], kv4.at[v, e0], r4.at[v, e0], dev(z, h, other))

        def to_edge():
            return pltpu.make_async_remote_copy(
                src_ref=kv4.at[v, e0], dst_ref=kv4.at[v, e1], send_sem=ssem.at[152 + v],
                recv_sem=r4.at[v, e1], device_id=dev(z, edge, k), device_id_type=MESH,
            )

        def to_partner():
            return pltpu.make_async_remote_copy(
                src_ref=kv4.at[v, e1], dst_ref=kv4.at[v, e1], send_sem=ssem.at[154 + v],
                recv_sem=r4.at[v, e1], device_id=dev(z, h, other), device_id_type=MESH,
            )

        @pl.when(inner)
        def _():
            to_edge().start()

        @pl.when(outer)
        def _():
            arrived(kv4.at[v, e1], r4.at[v, e1])
            to_partner().start()

    for v in range(2):
        for dz in (-1, 0, 1):
            for hp in range(CHIPS):
                slot = u_slot(8 * dz + 2 * hp + other, k)
                arrived(kvu.at[v, slot], ru.at[v, slot])
                slot = 8 + 8 * dz + 2 * hp + other
                arrived(kv4.at[v, slot], r4.at[v, slot])
        for i in range(4):
            arrived(kvu.at[v, 24 * k + i], ru.at[v, 24 * k + i])
        arrived(kv4.at[v, 24 + other], r4.at[v, 24 + other])

        @pl.when(outer)
        def _():
            arrived(kv4.at[v, 26 + other], r4.at[v, 26 + other])

    for i in range(4):
        arrived(qu.at[i], rq.at[i])
        arrived(adju.at[i], ra.at[i])

    for copy in sends:
        copy.wait_send()
    for copy in locals_:
        copy.wait()

    @pl.when(jnp.logical_not(to_self))
    def _():
        for n, (src, dst, sem) in enumerate(own_q):
            pltpu.make_async_copy(src, src, ssem.at[150 + n]).wait()

    for v in range(2):
        @pl.when(inner)
        def _():
            pltpu.make_async_copy(kv4.at[v, 24 + k], kv4.at[v, 24 + k], ssem.at[152 + v]).wait()

        @pl.when(outer)
        def _():
            pltpu.make_async_copy(kv4.at[v, 26 + k], kv4.at[v, 26 + k], ssem.at[154 + v]).wait()


def gather(q_in, k_in, v_in, q_gain, k_gain, adjacent):
    any_space = pl.BlockSpec(memory_space=pl.ANY)
    vmem = pl.BlockSpec(memory_space=pltpu.VMEM)
    bf16 = jnp.bfloat16
    dma = pltpu.SemaphoreType.DMA
    return pl.pallas_call(
        gather_kernel,
        name="gather_window",
        out_shape=(
            jax.ShapeDtypeStruct((2, SLOTS, TOK, HD), bf16),
            jax.ShapeDtypeStruct((2, SLOTS, TOK, HD), bf16),
            jax.ShapeDtypeStruct((4, TOK, HD), bf16),
            jax.ShapeDtypeStruct((TOK, HD), bf16),
            jax.ShapeDtypeStruct((4, 2, 128), jnp.int32),
        ),
        in_specs=[vmem] * 6,
        out_specs=(any_space,) * 5,
        scratch_shapes=[
            pltpu.VMEM((HEADS, TOK, HD), bf16),
            pltpu.VMEM((HEADS, TOK, HD), bf16),
            pltpu.VMEM((8, 128), jnp.float32),
            pltpu.VMEM((TENSOR, 8, 128), jnp.float32),
            pltpu.VMEM((3, TOK, HD), bf16),
            dma((160,)),
            dma((8,)),
            dma((2, SLOTS)),
            dma((2, SLOTS)),
            dma((4,)),
            dma((4,)),
            dma((3,)),
            dma((TENSOR,)),
        ],
        compiler_params=pltpu.CompilerParams(collective_id=0, has_side_effects=True),
    )(q_in, k_in, v_in, q_gain, k_gain, adjacent)


def attend_kernel(frames, adj, adju, qu, q4, kvu, kv4, ou, o4, m_sc, l_sc, acc_sc):
    z, h, k, _ = place()
    lane = lax.broadcasted_iota(jnp.int32, (1, TOK), 1)

    def sweep(q_of, adj_of, s_q, begin, count, key_shard, kv, finish):
        m_sc[...] = jnp.full_like(m_sc, -3e38)
        l_sc[...] = jnp.zeros_like(l_sc)
        acc_sc[...] = jnp.zeros_like(acc_sc)
        fq = [frames[2 * s_q + a] for a in range(2)]

        def tile(n, carry):
            slot = begin + n
            s_k = key_shard(slot)
            valid = jnp.logical_and(s_k >= 0, s_k < 64)
            s_k = jnp.clip(s_k, 0, 63)
            fine = []
            for a in range(2):
                for b in range(2):
                    gap = jnp.abs(fq[a] - frames[2 * s_k + b])
                    near = jnp.logical_and(gap == 1, adj_of(a, 2 * s_k + b) == 1)
                    fine.append(jnp.where(jnp.logical_and(valid, jnp.logical_or(gap == 0, near)), 1, 0))
            @pl.when(fine[0] + fine[1] + fine[2] + fine[3] > 0)
            def _():
                key = kv[1, slot]
                value = kv[0, slot]
                for a in range(2):
                    rows = slice(a * 128, (a + 1) * 128)
                    bias = jnp.where(
                        lane < 128,
                        jnp.where(fine[2 * a] > 0, 0.0, BLOCKED),
                        jnp.where(fine[2 * a + 1] > 0, 0.0, BLOCKED),
                    )
                    s = lax.dot_general(
                        q_of(rows), key, (((1,), (1,)), ((), ())),
                        preferred_element_type=jnp.float32,
                    )
                    s = s * EXP2_SCALE + bias
                    old = m_sc[rows, :]
                    new = jnp.maximum(old, jnp.max(s, axis=1, keepdims=True))
                    fade = jnp.exp2(old - new)
                    p = jnp.exp2(s - new[:, :1])
                    m_sc[rows, :] = new
                    l_sc[rows, :] = l_sc[rows, :] * fade + jnp.sum(p, axis=1, keepdims=True)
                    acc_sc[rows, :] = acc_sc[rows, :] * fade + jnp.dot(
                        p.astype(jnp.bfloat16), value, preferred_element_type=jnp.float32
                    )
            return carry

        lax.fori_loop(0, count, tile, 0)
        finish(acc_sc[...] / l_sc[...])

    def body(i, carry):
        def finish(x):
            ou[i] = x.astype(jnp.bfloat16)

        sweep(
            lambda rows: qu[i, rows, :],
            lambda a, block: adju[i, a, block],
            8 * z + 4 * k + i,
            i,
            25,
            lambda slot: 8 * z + 4 * k + slot - 12,
            kvu,
            finish,
        )
        return carry

    lax.fori_loop(0, 4, body, 0)

    def key_shard(slot):
        side = jnp.where(h < 2, -2, 2)
        e0 = 8 * (z + side) + 2 * lax.rem(h + 2, CHIPS) + slot - 24
        e1 = jnp.where(h == 0, 8 * (z - 2) + 6, jnp.where(h == 3, 8 * (z + 2), -1000)) + slot - 26
        return jnp.where(slot < 24, 8 * z - 8 + slot, jnp.where(slot < 26, e0, e1))

    def finish4(x):
        o4[...] = x

    sweep(
        lambda rows: q4[rows, :],
        lambda a, block: adj[a, block],
        8 * z + 2 * h + k,
        0,
        SLOTS,
        key_shard,
        kv4,
        finish4,
    )


def attend(frames, adjacent, adju, qu, q4, kvu, kv4):
    vmem = pl.BlockSpec(memory_space=pltpu.VMEM)
    smem = pl.BlockSpec(memory_space=pltpu.SMEM)
    return pl.pallas_call(
        attend_kernel,
        name="attend",
        out_shape=(
            jax.ShapeDtypeStruct((4, TOK, HD), jnp.bfloat16),
            jax.ShapeDtypeStruct((TOK, HD), jnp.float32),
        ),
        in_specs=[smem] * 3 + [vmem] * 4,
        out_specs=(vmem, vmem),
        scratch_shapes=[pltpu.VMEM((TOK, HD), jnp.float32)] * 3,
    )(frames, adjacent, adju, qu, q4, kvu, kv4)


def return_kernel(ou, o4, out, rbuf, ssem, rsem):
    z, h, k, t = place()
    other = 1 - k

    def dev(hh, kk):
        return (z * 8 + hh * 2 + kk, t)

    def chip(step):
        return lax.rem(h + step, CHIPS)

    barrier = pltpu.get_barrier_semaphore()
    peers = [dev(h, other)]
    for step in (1, 2, 3):
        peers += [dev(chip(step), 0), dev(chip(step), 1)]
    for peer in peers:
        pl.semaphore_signal(barrier, inc=1, device_id=peer, device_id_type=MESH)
    out[:, 4 * HD :] = o4[...]
    pl.semaphore_wait(barrier, len(peers))

    for i in range(4):
        hh, kk = 2 * k + i // 2, i % 2
        mine = jnp.logical_and(hh == h, kk == k)

        @pl.when(mine)
        def _():
            pltpu.make_async_copy(ou.at[i], rbuf.at[h], rsem.at[h]).start()

        @pl.when(jnp.logical_not(mine))
        def _():
            pltpu.make_async_remote_copy(
                src_ref=ou.at[i], dst_ref=rbuf.at[h], send_sem=ssem.at[i], recv_sem=rsem.at[h],
                device_id=dev(hh, kk), device_id_type=MESH,
            ).start()

    for i in range(4):
        pltpu.make_async_copy(rbuf.at[i], rbuf.at[i], rsem.at[i]).wait()
        out[:, i * HD : (i + 1) * HD] = rbuf[i].astype(jnp.float32)

    for i in range(4):
        hh, kk = 2 * k + i // 2, i % 2
        mine = jnp.logical_and(hh == h, kk == k)

        @pl.when(jnp.logical_not(mine))
        def _():
            pltpu.make_async_copy(ou.at[i], ou.at[i], ssem.at[i]).wait()


def give_back(ou, o4):
    vmem = pl.BlockSpec(memory_space=pltpu.VMEM)
    return pl.pallas_call(
        return_kernel,
        name="give_back",
        out_shape=jax.ShapeDtypeStruct((TOK, HEADS * HD), jnp.float32),
        in_specs=[vmem] * 2,
        out_specs=vmem,
        scratch_shapes=[
            pltpu.VMEM((4, TOK, HD), jnp.bfloat16),
            pltpu.SemaphoreType.DMA((4,)),
            pltpu.SemaphoreType.DMA((4,)),
        ],
        compiler_params=pltpu.CompilerParams(collective_id=1, has_side_effects=True),
    )(ou, o4)


def shards(q_in, k_in, v_in, q_gain, k_gain, frames, adjacent):
    kvu, kv4, qu, q4, adju = gather(
        q_in, k_in, v_in, q_gain[None, :], k_gain[None, :], adjacent
    )
    ou, o4 = attend(frames, adjacent, adju, qu, q4, kvu, kv4)
    return give_back(ou, o4)


def solution(mesh):
    return jax.shard_map(
        shards,
        mesh=mesh,
        in_specs=(
            P("seq", "tensor"),
            P("seq", "tensor"),
            P("seq", "tensor"),
            P("tensor"),
            P("tensor"),
            P(),
            P("seq", None),
        ),
        out_specs=P("seq", "tensor"),
        check_vma=False,
    )
```

time: 692 us -> 159 us (0.23)
  the two profiles are of different devices: /device:TPU:266 before, /device:TPU:245 now
where the time goes in v1:
time: 159 us
  Pallas kernels  155 us (97%)
  local copies, waits for them, and re-layouts  4.49 us (3%)
    pallas_call x1, Pallas kernels, attend(): pl.pallas_call(attend_kernel, name='attend', out_shape=(jax.ShapeDtypeStr...  78 us
    pallas_call x1, Pallas kernels, gather(): pl.pallas_call(gather_kernel, name='gather_window', out_shape=(jax.ShapeD...  63.7 us
    pallas_call x1, Pallas kernels, give_back(): pl.pallas_call(return_kernel, name='give_back', out_shape=jax.ShapeDtypeS...  13.2 us

profile of v1, /device:TPU:245, one launch (start us, length us, event | category | flops | bytes accessed | tf_op | source)
XLA Modules:
  0.0 159.4 jit_solution(16250324956601562201)
XLA Ops:
  0.0 1.3 broadcast_in_dim.6.qg_ref
  1.3 1.3 broadcast_in_dim.7.kg_ref
  2.5 63.7 %gather_window.1 = (bf16[2,28,256,128]{3,2,1,0:T(8,128)(2,1)}, bf16[2,28,256,128]{3,2,1,0:T(8,128)(2,1)}, bf16[4,256,128]{2,1,0:T(8,128)(2,1)}, bf16[256,128]{1,0:T(8,128)(2,1)}, s32[4,2,128]{2,1,0:T(2,128)}) custom-call(f32[256,640]{1,0:T(8,128)} %q_ref.1, f32[256,640]{1,0:T(8,128)} %k_ref.1, bf16[256,640]{1,0:T(8,128)(2,1)} %v_ref.1, ...), custom_call_target="tpu_custom_call" | custom-call | tf_op jit(solution)/shard_map/gather_window/pallas_call | solution.py:309
  66.3 78.0 %attend.1 = (bf16[4,256,128]{2,1,0:T(8,128)(2,1)}, f32[256,128]{1,0:T(8,128)}) custom-call(s32[128]{0:T(128)} %frames.1, s32[2,128]{1,0:T(2,128)} %adj.1, s32[4,2,128]{2,1,0:T(2,128)} %get-tuple-element.12.adju, bf16[4,256,128]{2,1,0:T(8,128)(2,1)} %get-tuple-element.13.qu, bf16[256,128]{1,0:T(8,128)(2,1)} %get-tuple-element.14.q4, ...), custom_call_target="tpu_custom_call" | custom-call | tf_op jit(solution)/shard_map/attend/pallas_call | solution.py:433
  144.2 13.2 %give_back.1 = f32[256,640]{1,0:T(8,128)} custom-call(bf16[4,256,128]{2,1,0:T(8,128)(2,1)} %get-tuple-element.17.ou, f32[256,128]{1,0:T(8,128)} %get-tuple-element.18.o4), custom_call_target="tpu_custom_call" | custom-call | tf_op jit(solution)/shard_map/give_back/pallas_call | solution.py:495
  157.4 2.0 %copy.9 = f32[256,640]{1,0:T(8,128)} copy(f32[256,640]{1,0:T(8,128)} %give_back.1) | data formatting | bytes 1310720

commit v2 on v1

v2 whole, which is shorter than its diff:
```python
import math

import jax
import jax.numpy as jnp
from jax import lax
from jax.experimental import pallas as pl
from jax.experimental.pallas import tpu as pltpu
from jax.sharding import PartitionSpec as P

HD = 128
TOK = 256
HEADS = 5
CHIPS = 4
PLANES = 8
TENSOR = 8
SLOTS = 28
MESH = pl.DeviceIdType.MESH
EPS = 1e-06
BLOCKED = -1e30
EXP2_SCALE = math.log2(math.e) / math.sqrt(HD)


def place():
    s = lax.axis_index("seq")
    return lax.div(s, 8), lax.rem(lax.div(s, 2), 4), lax.rem(s, 2), lax.axis_index("tensor")


def gather_kernel(
    q_ref, k_ref, v_ref, qg_ref, kg_ref, adj_ref,
    vu, ku, v4, k4, qu, q4, adju,
    qn, kn, vt, stat, statr, relay_v, relay_k, relay_q,
    ssem, lsem, ru, r4, rq, ra, rrelay, rstat,
):
    z, h, k, t = place()
    other = 1 - k
    kvu, kv4 = (vu, ku), (v4, k4)
    relay = (relay_v, relay_k, relay_q)

    def dev(zz, hh, kk):
        return (lax.rem(zz + PLANES, PLANES) * 8 + hh * 2 + kk, t)

    def chip(step):
        return lax.rem(h + step, CHIPS)

    sends = []
    locals_ = []

    def send(src, dst, rsem, device):
        copy = pltpu.make_async_remote_copy(
            src_ref=src, dst_ref=dst, send_sem=ssem.at[len(sends)], recv_sem=rsem,
            device_id=device, device_id_type=MESH,
        )
        sends.append(copy)
        copy.start()
        return copy

    def local(src, dst):
        copy = pltpu.make_async_copy(src, dst, lsem.at[len(locals_)])
        locals_.append(copy)
        copy.start()

    def arrived(dst, rsem):
        pltpu.make_async_copy(dst, dst, rsem).wait()

    barrier = pltpu.get_barrier_semaphore()
    peers = [dev(z, h, other)]
    for step in (1, 2, 3):
        peers += [dev(z, chip(step), 0), dev(z, chip(step), 1)]
    for zz in (z + 1, z - 1):
        peers += [dev(zz, h, 0), dev(zz, h, 1)]
    s_me = lax.axis_index("seq")
    for step in range(1, TENSOR):
        peers.append((s_me, lax.rem(t + step, TENSOR)))
    for peer in peers:
        pl.semaphore_signal(barrier, inc=1, device_id=peer, device_id_type=MESH)

    eye = lax.broadcasted_iota(jnp.int32, (128, 128), 0) == lax.broadcasted_iota(
        jnp.int32, (128, 128), 1
    )
    rows = []
    for ref in (q_ref, k_ref):
        for half in range(2):
            part = ref[half * 128 : (half + 1) * 128, :]
            column = jnp.sum(part * part, axis=1, keepdims=True)
            rows.append(jnp.sum(jnp.where(eye, column, 0.0), axis=0, keepdims=True))
    mine = jnp.concatenate(rows + [jnp.zeros((4, 128), jnp.float32)], axis=0)
    stat[...] = mine
    statr[t] = mine
    for i in range(HEADS):
        vt[i] = v_ref[:, i * HD : (i + 1) * HD].T

    pl.semaphore_wait(barrier, len(peers))

    for step in range(1, TENSOR):
        send(stat, statr.at[t], rstat.at[t], (s_me, lax.rem(t + step, TENSOR)))

    def u_slot(position, core):
        return position + 12 - 4 * core

    def spread_u(v, hp, src):
        p = 2 * hp + k
        slot = u_slot(p, other)
        send(src, kvu[v].at[u_slot(p - 8, k)], ru.at[v, u_slot(p - 8, k)], dev(z + 1, h, k))
        send(src, kvu[v].at[u_slot(p + 8, k)], ru.at[v, u_slot(p + 8, k)], dev(z - 1, h, k))
        send(src, kvu[v].at[slot], ru.at[v, slot], dev(z, h, other))

    def spread_4(v, hp, src):
        slot = 8 + 2 * hp + k
        send(src, kv4[v].at[slot - 8], r4.at[v, slot - 8], dev(z + 1, h, k))
        send(src, kv4[v].at[slot + 8], r4.at[v, slot + 8], dev(z - 1, h, k))
        send(src, kv4[v].at[slot], r4.at[v, slot], dev(z, h, other))

    own = 2 * h + k
    relay_to = {0: (1, 0), 1: (3, 1)}

    def first(v, head):
        side, buf = relay_to[v]
        slot = u_slot(own, k)
        send(head(chip(2)), relay[buf], rrelay.at[buf], dev(z, chip(side), k))
        for step in (1, 3):
            send(head(chip(step)), kvu[v].at[slot], ru.at[v, slot], dev(z, chip(step), k))
        spread_u(v, h, head(h))
        for step in (1, 3):
            send(head(4), kv4[v].at[8 + own], r4.at[v, 8 + own], dev(z, chip(step), k))
        spread_4(v, h, head(4))
        local(head(h), kvu[v].at[slot])
        local(head(4), kv4[v].at[8 + own])

    first(0, lambda i: vt.at[i])

    for step in range(1, TENSOR):
        j = lax.rem(t + step, TENSOR)
        arrived(statr.at[j], rstat.at[j])
    total = statr[0]
    for j in range(1, TENSOR):
        total = total + statr[j]
    inverse = 1.0 / jnp.sqrt(total / float(HD * HEADS * TENSOR) + EPS)
    for row, ref, gain in ((2, k_ref, kg_ref), (0, q_ref, qg_ref)):
        for half in range(2):
            lane_row = inverse[row + half : row + half + 1, :]
            column = jnp.sum(jnp.where(eye, lane_row, 0.0), axis=1, keepdims=True)
            span = slice(half * 128, (half + 1) * 128)
            for i in range(HEADS):
                feature = slice(i * HD, (i + 1) * HD)
                part = ref[span, feature] * column * gain[feature][None, :]
                if row == 2:
                    kn[i, span, :] = part.astype(jnp.bfloat16)
                else:
                    qn[i, :, span] = part.T.astype(jnp.bfloat16)

    first(1, lambda i: kn.at[i])

    core = lax.div(h, 2)
    place_q = 2 * lax.rem(h, 2) + k
    side_q = chip(1 + 2 * k)
    send(qn.at[chip(2)], relay[2], rrelay.at[2], dev(z, side_q, k))
    for step in (1, 3):
        send(qn.at[chip(step)], qu.at[place_q], rq.at[place_q], dev(z, chip(step), core))
    for step in (1, 2, 3):
        send(adj_ref, adju.at[place_q], ra.at[place_q], dev(z, chip(step), core))
    to_self = core == k
    own_q = [
        (qn.at[h], qu.at[place_q], rq.at[place_q]),
        (adj_ref, adju.at[place_q], ra.at[place_q]),
    ]
    cross = len(sends)
    for n, (src, dst, sem) in enumerate(own_q):
        @pl.when(to_self)
        def _():
            pltpu.make_async_copy(src, dst, sem).start()

        @pl.when(jnp.logical_not(to_self))
        def _():
            pltpu.make_async_remote_copy(
                src_ref=src, dst_ref=dst, send_sem=ssem.at[150 + n], recv_sem=sem,
                device_id=dev(z, h, other), device_id_type=MESH,
            ).start()
    local(qn.at[4], q4)

    for v in range(2):
        side, buf = relay_to[v]
        back = chip(4 - side)
        arrived(relay[buf], rrelay.at[buf])
        slot = u_slot(2 * back + k, k)
        send(relay[buf], kvu[v].at[slot], ru.at[v, slot], dev(z, chip(side), k))
        for step in (1, 3):
            hp = chip(step)
            slot = u_slot(2 * hp + k, k)
            arrived(kvu[v].at[slot], ru.at[v, slot])
            spread_u(v, hp, kvu[v].at[slot])
        for step in (4 - side, side):
            hp = chip(step)
            slot = 8 + 2 * hp + k
            arrived(kv4[v].at[slot], r4.at[v, slot])
            if step == 4 - side:
                send(kv4[v].at[slot], kv4[v].at[slot], r4.at[v, slot], dev(z, chip(side), k))
            spread_4(v, hp, kv4[v].at[slot])
        hp = chip(2)
        slot = u_slot(2 * hp + k, k)
        arrived(kvu[v].at[slot], ru.at[v, slot])
        spread_u(v, hp, kvu[v].at[slot])
        slot = 8 + 2 * hp + k
        arrived(kv4[v].at[slot], r4.at[v, slot])
        spread_4(v, hp, kv4[v].at[slot])

    source = chip(3 - 2 * k)
    arrived(relay[2], rrelay.at[2])
    where_q = 2 * lax.rem(source, 2) + k
    send(
        relay[2], qu.at[where_q], rq.at[where_q],
        dev(z, lax.rem(source + 2, CHIPS), lax.div(source, 2)),
    )

    for step in (0, 1, 3, 2):
        hp = chip(step)
        up = lax.div(hp, 2)
        sign = 1 - 2 * up
        for v in range(2):
            p = 2 * hp + k
            for q in (p - 8, p + 8):
                slot = u_slot(q, k)
                arrived(kvu[v].at[slot], ru.at[v, slot])
                slot_other = u_slot(q, other)
                send(kvu[v].at[slot], kvu[v].at[slot_other], ru.at[v, slot_other], dev(z, h, other))
            target = u_slot(p + 16 * sign, 1 - up)
            send(
                kvu[v].at[u_slot(p + 8 * sign, k)], kvu[v].at[target], ru.at[v, target],
                dev(z - sign, h, 1 - up),
            )
            for slot in (2 * hp + k, 16 + 2 * hp + k):
                arrived(kv4[v].at[slot], r4.at[v, slot])
                send(kv4[v].at[slot], kv4[v].at[slot], r4.at[v, slot], dev(z, h, other))
            if step == 2:
                send(
                    kv4[v].at[8 + 8 * sign + 2 * hp + k], kv4[v].at[24 + k], r4.at[v, 24 + k],
                    dev(z - sign, h, k),
                )

    inner = jnp.logical_or(h == 1, h == 2)
    outer = jnp.logical_or(h == 0, h == 3)
    edge = lax.div(h, 2) * 3
    for v in range(2):
        e0, e1 = 24 + k, 26 + k
        arrived(kv4[v].at[e0], r4.at[v, e0])
        send(kv4[v].at[e0], kv4[v].at[e0], r4.at[v, e0], dev(z, h, other))

        def to_edge():
            return pltpu.make_async_remote_copy(
                src_ref=kv4[v].at[e0], dst_ref=kv4[v].at[e1], send_sem=ssem.at[152 + v],
                recv_sem=r4.at[v, e1], device_id=dev(z, edge, k), device_id_type=MESH,
            )

        def to_partner():
            return pltpu.make_async_remote_copy(
                src_ref=kv4[v].at[e1], dst_ref=kv4[v].at[e1], send_sem=ssem.at[154 + v],
                recv_sem=r4.at[v, e1], device_id=dev(z, h, other), device_id_type=MESH,
            )

        @pl.when(inner)
        def _():
            to_edge().start()

        @pl.when(outer)
        def _():
            arrived(kv4[v].at[e1], r4.at[v, e1])
            to_partner().start()

    for v in range(2):
        for dz in (-1, 0, 1):
            for hp in range(CHIPS):
                slot = u_slot(8 * dz + 2 * hp + other, k)
                arrived(kvu[v].at[slot], ru.at[v, slot])
                slot = 8 + 8 * dz + 2 * hp + other
                arrived(kv4[v].at[slot], r4.at[v, slot])
        for i in range(4):
            arrived(kvu[v].at[24 * k + i], ru.at[v, 24 * k + i])
        arrived(kv4[v].at[24 + other], r4.at[v, 24 + other])

        @pl.when(outer)
        def _():
            arrived(kv4[v].at[26 + other], r4.at[v, 26 + other])

    for i in range(4):
        arrived(qu.at[i], rq.at[i])
        arrived(adju.at[i], ra.at[i])

    for copy in sends:
        copy.wait_send()
    for copy in locals_:
        copy.wait()

    @pl.when(jnp.logical_not(to_self))
    def _():
        for n, (src, dst, sem) in enumerate(own_q):
            pltpu.make_async_copy(src, src, ssem.at[150 + n]).wait()

    for v in range(2):
        @pl.when(inner)
        def _():
            pltpu.make_async_copy(kv4[v].at[24 + k], kv4[v].at[24 + k], ssem.at[152 + v]).wait()

        @pl.when(outer)
        def _():
            pltpu.make_async_copy(kv4[v].at[26 + k], kv4[v].at[26 + k], ssem.at[154 + v]).wait()


def gather(q_in, k_in, v_in, q_gain, k_gain, adjacent):
    any_space = pl.BlockSpec(memory_space=pl.ANY)
    vmem = pl.BlockSpec(memory_space=pltpu.VMEM)
    bf16 = jnp.bfloat16
    dma = pltpu.SemaphoreType.DMA
    return pl.pallas_call(
        gather_kernel,
        name="gather_window",
        out_shape=(
            jax.ShapeDtypeStruct((SLOTS, HD, TOK), bf16),
            jax.ShapeDtypeStruct((SLOTS, TOK, HD), bf16),
            jax.ShapeDtypeStruct((SLOTS, HD, TOK), bf16),
            jax.ShapeDtypeStruct((SLOTS, TOK, HD), bf16),
            jax.ShapeDtypeStruct((4, HD, TOK), bf16),
            jax.ShapeDtypeStruct((HD, TOK), bf16),
            jax.ShapeDtypeStruct((4, 2, 128), jnp.int32),
        ),
        in_specs=[vmem] * 6,
        out_specs=(any_space,) * 7,
        scratch_shapes=[
            pltpu.VMEM((HEADS, HD, TOK), bf16),
            pltpu.VMEM((HEADS, TOK, HD), bf16),
            pltpu.VMEM((HEADS, HD, TOK), bf16),
            pltpu.VMEM((8, 128), jnp.float32),
            pltpu.VMEM((TENSOR, 8, 128), jnp.float32),
            pltpu.VMEM((HD, TOK), bf16),
            pltpu.VMEM((TOK, HD), bf16),
            pltpu.VMEM((HD, TOK), bf16),
            dma((160,)),
            dma((8,)),
            dma((2, SLOTS)),
            dma((2, SLOTS)),
            dma((4,)),
            dma((4,)),
            dma((3,)),
            dma((TENSOR,)),
        ],
        compiler_params=pltpu.CompilerParams(collective_id=0, has_side_effects=True),
    )(q_in, k_in, v_in, q_gain, k_gain, adjacent)


def fold(tiles, m_sc, l_sc, acc_sc):
    halves = (slice(0, 128), slice(128, 256))
    for state, queries, keys, values, bias in tiles:
        scores = jnp.dot(keys, queries, preferred_element_type=jnp.float32)
        weights, news, sums = [], [], []
        for a in range(2):
            old = m_sc[state, :, halves[a]]
            new = old
            for b in range(2):
                top = jnp.max(scores[halves[b], halves[a]], axis=0, keepdims=True)
                new = jnp.maximum(new, top * EXP2_SCALE + bias[a][b])
            parts = [
                jnp.exp2(scores[halves[b], halves[a]] * EXP2_SCALE - (new - bias[a][b]))
                for b in range(2)
            ]
            column = jnp.concatenate(parts, axis=0)
            sums.append(jnp.sum(column, axis=0, keepdims=True))
            weights.append(column.astype(jnp.bfloat16))
            news.append(new)
        new = jnp.concatenate(news, axis=1)
        fade = jnp.exp2(m_sc[state] - new)
        m_sc[state] = new
        l_sc[state] = l_sc[state] * fade + jnp.concatenate(sums, axis=1)
        mixed = jnp.dot(
            values, jnp.concatenate(weights, axis=1), preferred_element_type=jnp.float32
        )
        acc_sc[state] = acc_sc[state] * fade + mixed


def attend_kernel(frames, adj, adju, qu, q4, vu, ku, v4, k4, ou, o4, bias_v, bias_s, sem, m_sc, l_sc, acc_sc):
    z, h, k, _ = place()

    frame_row = frames[...][None, :]
    lane = lax.broadcasted_iota(jnp.int32, (1, 128), 1)
    rows = []
    for i in range(5):
        shard = 8 * z + 4 * k + i if i < 4 else 8 * z + 2 * h + k
        for a in range(2):
            mine = jnp.max(jnp.where(lane == 2 * shard + a, frame_row, -1), axis=1, keepdims=True)
            gap = jnp.abs(frame_row - mine)
            linked = (adju[i, a : a + 1, :] if i < 4 else adj[a : a + 1, :]) == 1
            fine = (gap == 0) | ((gap == 1) & linked)
            rows.append(jnp.where(fine, 0.0, BLOCKED))
    bias_v[...] = jnp.concatenate(rows + [jnp.zeros((6, 128), jnp.float32)], axis=0)
    copy = pltpu.make_async_copy(bias_v, bias_s, sem)
    copy.start()
    m_sc[...] = jnp.full_like(m_sc, -1e29)
    l_sc[...] = jnp.zeros_like(l_sc)
    acc_sc[...] = jnp.zeros_like(acc_sc)
    copy.wait()

    def bias_of(i, shard):
        valid = jnp.logical_and(shard >= 0, shard < 64)
        at = jnp.clip(shard, 0, 63)
        return [
            [jnp.where(valid, bias_s[2 * i + a, 2 * at + b], BLOCKED) for b in range(2)]
            for a in range(2)
        ]

    def needed(biases):
        best = jnp.float32(BLOCKED)
        for bias in biases:
            for row in bias:
                for value in row:
                    best = jnp.maximum(best, value)
        return best == 0.0

    def u_group(slot, carry):
        shard = 8 * z + 4 * k + slot - 12
        biases = [bias_of(i, shard) for i in range(4)]

        @pl.when(needed(biases))
        def _():
            fold(
                [(i, qu[i], ku[slot], vu[slot], biases[i]) for i in range(4)],
                m_sc, l_sc, acc_sc,
            )

        return carry

    def key_shard(slot):
        side = jnp.where(h < 2, -2, 2)
        e0 = 8 * (z + side) + 2 * lax.rem(h + 2, CHIPS) + slot - 24
        e1 = jnp.where(h == 0, 8 * (z - 2) + 6, jnp.where(h == 3, 8 * (z + 2), -1000)) + slot - 26
        return jnp.where(slot < 24, 8 * z - 8 + slot, jnp.where(slot < 26, e0, e1))

    def h4_group(slot, carry):
        bias = bias_of(4, key_shard(slot))

        @pl.when(needed([bias]))
        def _():
            fold([(4, q4[...], k4[slot], v4[slot], bias)], m_sc, l_sc, acc_sc)

        return carry

    lax.fori_loop(0, SLOTS, u_group, 0)
    lax.fori_loop(0, SLOTS, h4_group, 0)
    for i in range(4):
        ou[i] = (acc_sc[i] / l_sc[i]).T.astype(jnp.bfloat16)
    o4[...] = (acc_sc[4] / l_sc[4]).T


def attend(frames, adjacent, adju, qu, q4, vu, ku, v4, k4):
    vmem = pl.BlockSpec(memory_space=pltpu.VMEM)
    f32 = jnp.float32
    return pl.pallas_call(
        attend_kernel,
        name="attend",
        out_shape=(
            jax.ShapeDtypeStruct((4, TOK, HD), jnp.bfloat16),
            jax.ShapeDtypeStruct((TOK, HD), f32),
        ),
        in_specs=[vmem] * 9,
        out_specs=(vmem, vmem),
        scratch_shapes=[
            pltpu.VMEM((16, 128), f32),
            pltpu.SMEM((16, 128), f32),
            pltpu.SemaphoreType.DMA,
            pltpu.VMEM((5, 1, TOK), f32),
            pltpu.VMEM((5, 1, TOK), f32),
            pltpu.VMEM((5, HD, TOK), f32),
        ],
    )(frames, adjacent, adju, qu, q4, vu, ku, v4, k4)


def return_kernel(ou, o4, out, rbuf, ssem, rsem):
    z, h, k, t = place()
    other = 1 - k

    def dev(hh, kk):
        return (z * 8 + hh * 2 + kk, t)

    def chip(step):
        return lax.rem(h + step, CHIPS)

    barrier = pltpu.get_barrier_semaphore()
    peers = [dev(h, other)]
    for step in (1, 2, 3):
        peers += [dev(chip(step), 0), dev(chip(step), 1)]
    for peer in peers:
        pl.semaphore_signal(barrier, inc=1, device_id=peer, device_id_type=MESH)
    out[:, 4 * HD :] = o4[...]
    pl.semaphore_wait(barrier, len(peers))

    for i in range(4):
        hh, kk = 2 * k + i // 2, i % 2
        mine = jnp.logical_and(hh == h, kk == k)

        @pl.when(mine)
        def _():
            pltpu.make_async_copy(ou.at[i], rbuf.at[h], rsem.at[h]).start()

        @pl.when(jnp.logical_not(mine))
        def _():
            pltpu.make_async_remote_copy(
                src_ref=ou.at[i], dst_ref=rbuf.at[h], send_sem=ssem.at[i], recv_sem=rsem.at[h],
                device_id=dev(hh, kk), device_id_type=MESH,
            ).start()

    for i in range(4):
        pltpu.make_async_copy(rbuf.at[i], rbuf.at[i], rsem.at[i]).wait()
        out[:, i * HD : (i + 1) * HD] = rbuf[i].astype(jnp.float32)

    for i in range(4):
        hh, kk = 2 * k + i // 2, i % 2
        mine = jnp.logical_and(hh == h, kk == k)

        @pl.when(jnp.logical_not(mine))
        def _():
            pltpu.make_async_copy(ou.at[i], ou.at[i], ssem.at[i]).wait()


def give_back(ou, o4):
    vmem = pl.BlockSpec(memory_space=pltpu.VMEM)
    return pl.pallas_call(
        return_kernel,
        name="give_back",
        out_shape=jax.ShapeDtypeStruct((TOK, HEADS * HD), jnp.float32),
        in_specs=[vmem] * 2,
        out_specs=vmem,
        scratch_shapes=[
            pltpu.VMEM((4, TOK, HD), jnp.bfloat16),
            pltpu.SemaphoreType.DMA((4,)),
            pltpu.SemaphoreType.DMA((4,)),
        ],
        compiler_params=pltpu.CompilerParams(collective_id=1, has_side_effects=True),
    )(ou, o4)


def shards(q_in, k_in, v_in, q_gain, k_gain, frames, adjacent):
    vu, ku, v4, k4, qu, q4, adju = gather(q_in, k_in, v_in, q_gain, k_gain, adjacent)
    ou, o4 = attend(frames, adjacent, adju, qu, q4, vu, ku, v4, k4)
    return give_back(ou, o4)


def solution(mesh):
    return jax.shard_map(
        shards,
        mesh=mesh,
        in_specs=(
            P("seq", "tensor"),
            P("seq", "tensor"),
            P("seq", "tensor"),
            P("tensor"),
            P("tensor"),
            P(),
            P("seq", None),
        ),
        out_specs=P("seq", "tensor"),
        check_vma=False,
    )
```

time: 159 us -> 124 us (0.78)
  the two profiles are of different devices: /device:TPU:245 before, /device:TPU:69 now
where the time goes in v2:
time: 124 us
  Pallas kernels  122 us (98%)
  local copies, waits for them, and re-layouts  1.97 us (2%)
    pallas_call x1, Pallas kernels, gather(): pl.pallas_call(gather_kernel, name='gather_window', out_shape=(jax.ShapeD...  67.9 us
    pallas_call x1, Pallas kernels, attend(): pl.pallas_call(attend_kernel, name='attend', out_shape=(jax.ShapeDtypeStr...  37.6 us
    pallas_call x1, Pallas kernels, give_back(): pl.pallas_call(return_kernel, name='give_back', out_shape=jax.ShapeDtypeS...  16.5 us

profile of v2, /device:TPU:69, one launch (start us, length us, event | category | flops | bytes accessed | tf_op | source)
XLA Modules:
  0.0 124.1 jit_solution(17491764581841676887)
XLA Ops:
  0.0 67.9 %gather_window.1 = (bf16[28,128,256]{2,1,0:T(8,128)(2,1)}, bf16[28,256,128]{2,1,0:T(8,128)(2,1)}, bf16[28,128,256]{2,1,0:T(8,128)(2,1)}, bf16[28,256,128]{2,1,0:...) custom-call(f32[256,640]{1,0:T(8,128)} %q_ref.1, f32[256,640]{1,0:T(8,128)} %k_ref.1, ...), custom_call_target="tpu_custom_call" | custom-call | tf_op jit(solution)/shard_map/gather_window/pallas_call | solution.py:312
  67.9 37.6 %attend.1 = (bf16[4,256,128]{2,1,0:T(8,128)(2,1)}, f32[256,128]{1,0:T(8,128)}) custom-call(s32[128]{0:T(128)} %frames.1, s32[2,128]{1,0:T(2,128)} %adj.1, s32[4,2,128]{2,1,0:T(2,128)} %get-tuple-element.14.adju, bf16[4,128,256]{2,1,0:T(8,128)(2,1)} %get-tuple-element.15.qu, bf16[128,256]{1,0:T(8,128)(2,1)} %get-tuple-element.16.q4, ...), custom_call_target="tpu_custom_call" | custom-call | tf_op jit(solution)/shard_map/attend/pallas_call | solution.py:453
  105.6 16.5 %give_back.1 = f32[256,640]{1,0:T(8,128)} custom-call(bf16[4,256,128]{2,1,0:T(8,128)(2,1)} %get-tuple-element.21.ou, f32[256,128]{1,0:T(8,128)} %get-tuple-element.22.o4), custom_call_target="tpu_custom_call" | custom-call | tf_op jit(solution)/shard_map/give_back/pallas_call | solution.py:522
  122.1 2.0 %copy.9 = f32[256,640]{1,0:T(8,128)} copy(f32[256,640]{1,0:T(8,128)} %give_back.1) | data formatting | bytes 1310720

commit v3 on v0

v3 whole, which is shorter than its diff:
```python
import math

import jax
import jax.numpy as jnp
from jax import lax
from jax.experimental import pallas as pl
from jax.experimental.pallas import tpu as pltpu
from jax.sharding import PartitionSpec as P

HD = 128
TOK = 256
HEADS = 5
CHIPS = 4
PLANES = 8
TENSOR = 8
SLOTS = 28
MESH = pl.DeviceIdType.MESH
EPS = 1e-06
BLOCKED = -1e30
EXP2_SCALE = math.log2(math.e) / math.sqrt(HD)


def place():
    s = lax.axis_index("seq")
    return lax.div(s, 8), lax.rem(lax.div(s, 2), 4), lax.rem(s, 2), lax.axis_index("tensor")


def fold(tiles, m_sc, l_sc, acc_sc):
    halves = (slice(0, 128), slice(128, 256))
    count = len(tiles)
    scores, weights, fades, sums = {}, {}, {}, {}

    def score(n):
        state, queries, keys, values, bias = tiles[n]
        scores[n] = jnp.dot(keys, queries, preferred_element_type=jnp.float32)

    def weigh(n):
        state, queries, keys, values, bias = tiles[n]
        s = scores.pop(n)
        blocks = s.shape[0] // 128
        columns, news, totals = [], [], []
        for a in range(2):
            new = m_sc[state, :, halves[a]]
            for b in range(blocks):
                top = jnp.max(s[b * 128 : (b + 1) * 128, halves[a]], axis=0, keepdims=True)
                new = jnp.maximum(new, top * EXP2_SCALE + bias[a][b])
            parts = [
                jnp.exp2(s[b * 128 : (b + 1) * 128, halves[a]] * EXP2_SCALE - (new - bias[a][b]))
                for b in range(blocks)
            ]
            column = jnp.concatenate(parts, axis=0)
            totals.append(jnp.sum(column, axis=0, keepdims=True))
            columns.append(column.astype(jnp.bfloat16))
            news.append(new)
        new = jnp.concatenate(news, axis=1)
        fades[n] = jnp.exp2(m_sc[state] - new)
        m_sc[state] = new
        l_sc[state] = l_sc[state] * fades[n] + jnp.concatenate(totals, axis=1)
        weights[n] = jnp.concatenate(columns, axis=1)

    def mix(n):
        state, queries, keys, values, bias = tiles[n]
        mixed = jnp.dot(values, weights.pop(n), preferred_element_type=jnp.float32)
        acc_sc[state] = acc_sc[state] * fades.pop(n) + mixed

    score(0)
    for n in range(count):
        if n + 1 < count:
            score(n + 1)
        if n > 0:
            mix(n - 1)
        weigh(n)
    mix(count - 1)


def kernel(
    q_ref, k_ref, v_ref, qg_ref, kg_ref, adj_ref, frames_ref,
    out_ref,
    vu, ku, v4, k4, qu, adju, qn, kn, vt, stat, statr, relay_v, relay_k, relay_q,
    bias_v, bias_s, m_sc, l_sc, acc_sc, obuf, rbuf,
    ssem, bsem, ru, r4, rq, ra, rrelay, rstat, ro,
):
    z, h, k, t = place()
    other = 1 - k
    kvu, kv4 = (vu, ku), (v4, k4)
    relay = (relay_v, relay_k, relay_q)
    s_me = lax.axis_index("seq")
    inner = jnp.logical_or(h == 1, h == 2)
    outer = jnp.logical_or(h == 0, h == 3)

    def dev(zz, hh, kk):
        return (lax.rem(zz + PLANES, PLANES) * 8 + hh * 2 + kk, t)

    def chip(step):
        return lax.rem(h + step, CHIPS)

    sends = []

    def send(src, dst, rsem, device):
        copy = pltpu.make_async_remote_copy(
            src_ref=src, dst_ref=dst, send_sem=ssem.at[len(sends)], recv_sem=rsem,
            device_id=device, device_id_type=MESH,
        )
        sends.append((copy, None))
        copy.start()

    def send_if(condition, src, dst, rsem, device):
        copy = pltpu.make_async_remote_copy(
            src_ref=src, dst_ref=dst, send_sem=ssem.at[len(sends)], recv_sem=rsem,
            device_id=device, device_id_type=MESH,
        )
        sends.append((copy, condition))

        @pl.when(condition)
        def _():
            copy.start()

    def arrived(dst, rsem):
        pltpu.make_async_copy(dst, dst, rsem).wait()

    for ref in (v4, k4):
        for slot in (26, 27):
            ref[slot] = jnp.zeros(ref.shape[1:], ref.dtype)

    barrier = pltpu.get_barrier_semaphore()
    peers = [dev(z, h, other)]
    for step in (1, 2, 3):
        peers += [dev(z, chip(step), 0), dev(z, chip(step), 1)]
    for zz in (z + 1, z - 1):
        peers += [dev(zz, h, 0), dev(zz, h, 1)]
    for step in range(1, TENSOR):
        peers.append((s_me, lax.rem(t + step, TENSOR)))
    for peer in peers:
        pl.semaphore_signal(barrier, inc=1, device_id=peer, device_id_type=MESH)

    eye = lax.broadcasted_iota(jnp.int32, (128, 128), 0) == lax.broadcasted_iota(
        jnp.int32, (128, 128), 1
    )
    rows = []
    for ref in (q_ref, k_ref):
        for half in range(2):
            part = ref[half * 128 : (half + 1) * 128, :]
            column = jnp.sum(part * part, axis=1, keepdims=True)
            rows.append(jnp.sum(jnp.where(eye, column, 0.0), axis=0, keepdims=True))
    mine = jnp.concatenate(rows + [jnp.zeros((4, 128), jnp.float32)], axis=0)
    stat[...] = mine
    statr[t] = mine

    def u_slot(position, core):
        return position + 12 - 4 * core

    own = 2 * h + k
    for i in range(HEADS):
        vt[i] = v_ref[:, i * HD : (i + 1) * HD].T
    vu[u_slot(own, k)] = vt[h]
    v4[8 + own] = vt[4]
    m_sc[...] = jnp.full_like(m_sc, -1e29)
    l_sc[...] = jnp.zeros_like(l_sc)
    acc_sc[...] = jnp.zeros_like(acc_sc)

    pl.semaphore_wait(barrier, len(peers))

    for step in range(1, TENSOR):
        send(stat, statr.at[t], rstat.at[t], (s_me, lax.rem(t + step, TENSOR)))

    def spread_u(v, hp, src):
        p = 2 * hp + k
        slot = u_slot(p, other)
        up, down = u_slot(p - 8, k), u_slot(p + 8, k)
        send(src, kvu[v].at[up], ru.at[v, up], dev(z + 1, h, k))
        send(src, kvu[v].at[down], ru.at[v, down], dev(z - 1, h, k))
        send(src, kvu[v].at[slot], ru.at[v, slot], dev(z, h, other))

    def spread_4(v, hp, src):
        slot = 8 + 2 * hp + k
        send(src, kv4[v].at[slot - 8], r4.at[v, slot - 8], dev(z + 1, h, k))
        send(src, kv4[v].at[slot + 8], r4.at[v, slot + 8], dev(z - 1, h, k))
        send(src, kv4[v].at[slot], r4.at[v, slot], dev(z, h, other))

    relay_to = {0: (1, 0), 1: (3, 1)}

    def first_y(v, ref):
        side, buf = relay_to[v]
        slot = u_slot(own, k)
        send(ref.at[chip(2)], relay[buf], rrelay.at[buf], dev(z, chip(side), k))
        for step in (1, 3):
            send(ref.at[chip(step)], kvu[v].at[slot], ru.at[v, slot], dev(z, chip(step), k))
        for step in (1, 3):
            send(ref.at[4], kv4[v].at[8 + own], r4.at[v, 8 + own], dev(z, chip(step), k))

    def first_z(v, ref):
        spread_u(v, h, ref.at[h])
        spread_4(v, h, ref.at[4])

    first_y(0, vt)
    first_z(0, vt)

    core = lax.div(h, 2)
    place_q = 2 * lax.rem(h, 2) + k
    to_self = core == k
    to_other = jnp.logical_not(to_self)
    for step in (1, 2, 3):
        send(adj_ref, adju.at[place_q], ra.at[place_q], dev(z, chip(step), core))
    send_if(to_other, adj_ref, adju.at[place_q], ra.at[place_q], dev(z, h, other))

    for step in range(1, TENSOR):
        j = lax.rem(t + step, TENSOR)
        arrived(statr.at[j], rstat.at[j])
    total = statr[0]
    for j in range(1, TENSOR):
        total = total + statr[j]
    inverse = 1.0 / jnp.sqrt(total / float(HD * HEADS * TENSOR) + EPS)

    def normalize(row, ref, gain, put):
        for half in range(2):
            lane_row = inverse[row + half : row + half + 1, :]
            column = jnp.sum(jnp.where(eye, lane_row, 0.0), axis=1, keepdims=True)
            span = slice(half * 128, (half + 1) * 128)
            for i in range(HEADS):
                feature = slice(i * HD, (i + 1) * HD)
                put(i, span, ref[span, feature] * column * gain[feature][None, :])

    def put_k(i, span, x):
        kn[i, span, :] = x.astype(jnp.bfloat16)

    def put_q(i, span, x):
        qn[i, :, span] = x.T.astype(jnp.bfloat16)

    normalize(2, k_ref, kg_ref, put_k)
    normalize(0, q_ref, qg_ref, put_q)
    ku[u_slot(own, k)] = kn[h]
    k4[8 + own] = kn[4]
    first_z(1, kn)

    send(qn.at[chip(2)], relay[2], rrelay.at[2], dev(z, chip(1 + 2 * k), k))
    for step in (1, 3):
        send(qn.at[chip(step)], qu.at[place_q], rq.at[place_q], dev(z, chip(step), core))
    send_if(to_other, qn.at[h], qu.at[place_q], rq.at[place_q], dev(z, h, other))

    @pl.when(to_self)
    def _():
        qu[place_q] = qn[h]
        adju[place_q] = adj_ref[...]

    first_y(1, kn)

    def pass_relay(v):
        side, buf = relay_to[v]
        arrived(relay[buf], rrelay.at[buf])
        slot = u_slot(2 * chip(4 - side) + k, k)
        send(relay[buf], kvu[v].at[slot], ru.at[v, slot], dev(z, chip(side), k))

    def plane_u(v, step):
        hp = chip(step)
        slot = u_slot(2 * hp + k, k)
        arrived(kvu[v].at[slot], ru.at[v, slot])
        spread_u(v, hp, kvu[v].at[slot])

    def plane_4(v, step):
        side = relay_to[v][0]
        hp = chip(step)
        slot = 8 + 2 * hp + k
        arrived(kv4[v].at[slot], r4.at[v, slot])
        if step == 4 - side:
            send(kv4[v].at[slot], kv4[v].at[slot], r4.at[v, slot], dev(z, chip(side), k))
        spread_4(v, hp, kv4[v].at[slot])

    def planes(v, step):
        hp = chip(step)
        sign = 1 - 2 * lax.div(hp, 2)
        p = 2 * hp + k
        for q in (p - 8, p + 8):
            slot = u_slot(q, k)
            arrived(kvu[v].at[slot], ru.at[v, slot])
        far = lax.div(1 + sign, 2)
        target = u_slot(p + 16 * sign, far)
        send(
            kvu[v].at[u_slot(p + 8 * sign, k)], kvu[v].at[target], ru.at[v, target],
            dev(z - sign, h, far),
        )
        for q in (p - 8, p + 8):
            to = u_slot(q, other)
            send(kvu[v].at[u_slot(q, k)], kvu[v].at[to], ru.at[v, to], dev(z, h, other))
        for slot in (p, 16 + p):
            arrived(kv4[v].at[slot], r4.at[v, slot])
        if step == 2:
            send(
                kv4[v].at[8 + 8 * sign + p], kv4[v].at[24 + k], r4.at[v, 24 + k],
                dev(z - sign, h, k),
            )
        for slot in (p, 16 + p):
            send(kv4[v].at[slot], kv4[v].at[slot], r4.at[v, slot], dev(z, h, other))

    def pass_query():
        source = chip(3 - 2 * k)
        arrived(relay[2], rrelay.at[2])
        where = 2 * lax.rem(source, 2) + k
        send(
            relay[2], qu.at[where], rq.at[where],
            dev(z, lax.rem(source + 2, CHIPS), lax.div(source, 2)),
        )

    def mine_q(i):
        return jnp.logical_and(to_self, place_q == i)

    def biases_ready():
        frame_row = frames_ref[...][None, :]
        lane = lax.broadcasted_iota(jnp.int32, (1, 128), 1)
        rows = []
        for i in range(5):
            if i < 4:
                @pl.when(jnp.logical_not(mine_q(i)))
                def _():
                    arrived(adju.at[i], ra.at[i])
            shard = 8 * z + 4 * k + i if i < 4 else s_me
            for a in range(2):
                at = jnp.where(lane == 2 * shard + a, frame_row, -1)
                gap = jnp.abs(frame_row - jnp.max(at, axis=1, keepdims=True))
                linked = (adju[i, a : a + 1, :] if i < 4 else adj_ref[a : a + 1, :]) == 1
                fine = (gap == 0) | ((gap == 1) & linked)
                rows.append(jnp.where(fine, 0.0, BLOCKED))
        bias_v[...] = jnp.concatenate(rows + [jnp.zeros((6, 128), jnp.float32)], axis=0)

    def bias_copy():
        return pltpu.make_async_copy(bias_v, bias_s, bsem)

    def bias_of(i, first_shard, second_shard):
        found = [[], []]
        for shard in (first_shard, second_shard):
            valid = jnp.logical_and(shard >= 0, shard < 64)
            at = jnp.clip(shard, 0, 63)
            for a in range(2):
                for b in range(2):
                    found[a].append(jnp.where(valid, bias_s[2 * i + a, 2 * at + b], BLOCKED))
        return found

    def unit(n, carry):
        step = jnp.where(n < 3, 0, jnp.where(n < 5, 2 * n - 5, jnp.where(n < 7, 1, jnp.where(n < 9, 3, 2))))
        turn = jnp.where(n < 3, n, jnp.where(n < 5, 0, jnp.where(n < 7, n - 4, jnp.where(n < 9, n - 6, n - 9))))
        dz = jnp.where(turn == 0, 0, 2 * turn - 3)
        far = n >= 12
        p = 8 * dz + 2 * lax.rem(h + step, CHIPS)
        slot = jnp.where(far, 24 * k + 2 * (n - 12), u_slot(p, k))
        slot4 = jnp.where(far, 24 + 2 * (n - 12), 8 + p)
        shard = 8 * z + 4 * k + slot - 12
        side = jnp.where(h < 2, -2, 2)
        e0 = 8 * (z + side) + 2 * lax.rem(h + 2, CHIPS)
        e1 = jnp.where(h == 0, 8 * (z - 2) + 6, jnp.where(h == 3, 8 * (z + 2), -1000))
        shard4 = jnp.where(n < 12, 8 * z + p, jnp.where(n == 12, e0, e1))
        tiles = []
        keys = ku[pl.ds(slot, 2)].reshape(2 * TOK, HD)
        values = jnp.concatenate([vu[slot], vu[slot + 1]], axis=1)
        for i in range(4):
            tiles.append((i, qu[i], keys, values, bias_of(i, shard, shard + 1)))
        keys = k4[pl.ds(slot4, 2)].reshape(2 * TOK, HD)
        values = jnp.concatenate([v4[slot4], v4[slot4 + 1]], axis=1)
        tiles.append((4, qn[4], keys, values, bias_of(4, shard4, shard4 + 1)))
        fold(tiles, m_sc, l_sc, acc_sc)
        return carry

    def from_partner(dz, step):
        for v in range(2):
            slot = u_slot(8 * dz + 2 * chip(step) + other, k)
            arrived(kvu[v].at[slot], ru.at[v, slot])
            slot = 8 + 8 * dz + 2 * chip(step) + other
            arrived(kv4[v].at[slot], r4.at[v, slot])

    def compute(begin, end):
        lax.fori_loop(begin, end, unit, 0)

    pass_relay(0)
    plane_u(0, 3)
    plane_u(0, 1)
    plane_4(0, 3)
    plane_4(0, 1)
    planes(0, 0)
    planes(1, 0)
    biases_ready()
    planes(0, 1)
    planes(0, 3)
    plane_u(0, 2)
    plane_4(0, 2)
    bias_copy().start()
    pass_query()
    pass_relay(1)
    plane_u(1, 3)
    plane_u(1, 1)
    plane_4(1, 1)
    plane_4(1, 3)
    planes(0, 2)
    bias_copy().wait()
    for i in range(4):
        @pl.when(jnp.logical_not(mine_q(i)))
        def _():
            arrived(qu.at[i], rq.at[i])
    for dz in (0, -1, 1):
        from_partner(dz, 0)
    compute(0, 2)
    planes(1, 1)
    planes(1, 3)
    plane_u(1, 2)
    plane_4(1, 2)
    for step in (1, 3):
        from_partner(0, step)
    compute(2, 5)
    planes(1, 2)
    for step in (1, 3):
        from_partner(-1, step)
        from_partner(1, step)
    compute(5, 7)
    edge = lax.div(h, 2) * 3
    for v in range(2):
        e0, e1 = 24 + k, 26 + k
        arrived(kv4[v].at[e0], r4.at[v, e0])
        send(kv4[v].at[e0], kv4[v].at[e0], r4.at[v, e0], dev(z, h, other))
        send_if(inner, kv4[v].at[e0], kv4[v].at[e1], r4.at[v, e1], dev(z, edge, k))
    from_partner(0, 2)
    compute(7, 10)
    for v in range(2):
        e1 = 26 + k

        @pl.when(outer)
        def _():
            arrived(kv4[v].at[e1], r4.at[v, e1])

        send_if(outer, kv4[v].at[e1], kv4[v].at[e1], r4.at[v, e1], dev(z, h, other))
    from_partner(-1, 2)
    from_partner(1, 2)
    for v in range(2):
        for i in range(4):
            arrived(kvu[v].at[24 * k + i], ru.at[v, 24 * k + i])
        arrived(kv4[v].at[24 + other], r4.at[v, 24 + other])

        @pl.when(outer)
        def _():
            arrived(kv4[v].at[26 + other], r4.at[v, 26 + other])
    compute(10, 14)

    def give(i):
        hh, kk = 2 * k + i // 2, i % 2
        away = jnp.logical_not(jnp.logical_and(hh == h, kk == k))
        send_if(away, obuf.at[i], rbuf.at[h], ro.at[h], dev(z, hh, kk))

        @pl.when(jnp.logical_not(away))
        def _():
            rbuf[h] = obuf[i]

    for i in range(4):
        obuf[i] = (acc_sc[i] / l_sc[i]).T.astype(jnp.bfloat16)
        if i > 0:
            give(i - 1)
    out_ref[:, 4 * HD :] = (acc_sc[4] / l_sc[4]).T
    give(3)
    for step in (0, 1, 3, 2):
        head = chip(step)
        if step == 0:
            @pl.when(to_other)
            def _():
                arrived(rbuf.at[head], ro.at[head])
        else:
            arrived(rbuf.at[head], ro.at[head])
    for i in range(4):
        out_ref[:, i * HD : (i + 1) * HD] = rbuf[i].astype(jnp.float32)

    for copy, condition in sends:
        if condition is None:
            copy.wait_send()
        else:
            pl.when(condition)(copy.wait_send)


def shards(q_in, k_in, v_in, q_gain, k_gain, frames, adjacent):
    vmem = pl.BlockSpec(memory_space=pltpu.VMEM)
    bf16, f32, dma = jnp.bfloat16, jnp.float32, pltpu.SemaphoreType.DMA
    return pl.pallas_call(
        kernel,
        name="window_attention",
        out_shape=jax.ShapeDtypeStruct((TOK, HEADS * HD), f32),
        in_specs=[vmem] * 7,
        out_specs=vmem,
        scratch_shapes=[
            pltpu.VMEM((SLOTS, HD, TOK), bf16),
            pltpu.VMEM((SLOTS, TOK, HD), bf16),
            pltpu.VMEM((SLOTS, HD, TOK), bf16),
            pltpu.VMEM((SLOTS, TOK, HD), bf16),
            pltpu.VMEM((4, HD, TOK), bf16),
            pltpu.VMEM((4, 2, 128), jnp.int32),
            pltpu.VMEM((HEADS, HD, TOK), bf16),
            pltpu.VMEM((HEADS, TOK, HD), bf16),
            pltpu.VMEM((HEADS, HD, TOK), bf16),
            pltpu.VMEM((8, 128), f32),
            pltpu.VMEM((TENSOR, 8, 128), f32),
            pltpu.VMEM((HD, TOK), bf16),
            pltpu.VMEM((TOK, HD), bf16),
            pltpu.VMEM((HD, TOK), bf16),
            pltpu.VMEM((16, 128), f32),
            pltpu.SMEM((16, 128), f32),
            pltpu.VMEM((5, 1, TOK), f32),
            pltpu.VMEM((5, 1, TOK), f32),
            pltpu.VMEM((5, HD, TOK), f32),
            pltpu.VMEM((4, TOK, HD), bf16),
            pltpu.VMEM((4, TOK, HD), bf16),
            dma((160,)),
            dma,
            dma((2, SLOTS)),
            dma((2, SLOTS)),
            dma((4,)),
            dma((4,)),
            dma((3,)),
            dma((TENSOR,)),
            dma((4,)),
        ],
        compiler_params=pltpu.CompilerParams(collective_id=0, has_side_effects=True),
    )(q_in, k_in, v_in, q_gain, k_gain, adjacent, frames)


def solution(mesh):
    return jax.shard_map(
        shards,
        mesh=mesh,
        in_specs=(
            P("seq", "tensor"),
            P("seq", "tensor"),
            P("seq", "tensor"),
            P("tensor"),
            P("tensor"),
            P(),
            P("seq", None),
        ),
        out_specs=P("seq", "tensor"),
        check_vma=False,
    )
```

time: 692 us -> 85.1 us (0.12)
  the two profiles are of different devices: /device:TPU:266 before, /device:TPU:1 now
where the time goes in v3:
time: 85.1 us; the launch traced here: 84.9 us
  Pallas kernels  82.9 us (97%)
  local copies, waits for them, and re-layouts  1.97 us (2%)
    pallas_call x1, Pallas kernels, shards(): pl.pallas_call(kernel, name='window_attention', out_shape=jax.ShapeDtypeS...  82.9 us
    unnamed x1, local copies, waits for them, and re-layouts  1.97 us

profile of v3, /device:TPU:1, one launch (start us, length us, event | category | flops | bytes accessed | tf_op | source)
XLA Modules:
  0.0 84.9 jit_solution(17417665811053209256)
XLA Ops:
  0.0 82.9 %window_attention.1 = f32[256,640]{1,0:T(8,128)} custom-call(f32[256,640]{1,0:T(8,128)} %q_ref.1, f32[256,640]{1,0:T(8,128)} %k_ref.1, bf16[256,640]{1,0:T(8,128)(2,1)} %v_ref.1, f32[640]{0:T(1024)} %qg_ref.1, f32[640]{0:T(1024)} %kg_ref.1, s32[2,128]{1,0:T(2,128)} %adj_ref.1, s32[128]{0:T(128)} %frames_ref.1), custom_call_target="tpu_custom_call" | custom-call | tf_op jit(solution)/shard_map/window_attention/pallas_call | solution.py:475
  82.9 2.0 %copy.9 = f32[256,640]{1,0:T(8,128)} copy(f32[256,640]{1,0:T(8,128)} %window_attention.1) | data formatting | bytes 1310720

commit v4 on v3

v4 whole, which is shorter than its diff:
```python
import math

import jax
import jax.numpy as jnp
from jax import lax
from jax.experimental import pallas as pl
from jax.experimental.pallas import tpu as pltpu
from jax.sharding import PartitionSpec as P

HD = 128
TOK = 256
HEADS = 5
CHIPS = 4
PLANES = 8
TENSOR = 8
SLOTS = 36
COLUMN = 28
MESH = pl.DeviceIdType.MESH
EPS = 1e-06
BLOCKED = -1e30
EXP2_SCALE = math.log2(math.e) / math.sqrt(HD)


def place():
    s = lax.axis_index("seq")
    return lax.div(s, 8), lax.rem(lax.div(s, 2), 4), lax.rem(s, 2), lax.axis_index("tensor")


def fold(tiles, m_sc, l_sc, acc_sc):
    halves = (slice(0, 128), slice(128, 256))
    count = len(tiles)
    scores, weights, fades, sums = {}, {}, {}, {}

    def score(n):
        state, queries, keys, values, bias = tiles[n]
        scores[n] = jnp.dot(keys, queries, preferred_element_type=jnp.float32)

    def weigh(n):
        state, queries, keys, values, bias = tiles[n]
        s = scores.pop(n)
        blocks = s.shape[0] // 128
        columns, news, totals = [], [], []
        for a in range(2):
            new = m_sc[state, :, halves[a]]
            for b in range(blocks):
                top = jnp.max(s[b * 128 : (b + 1) * 128, halves[a]], axis=0, keepdims=True)
                new = jnp.maximum(new, top * EXP2_SCALE + bias[a][b])
            parts = [
                jnp.exp2(s[b * 128 : (b + 1) * 128, halves[a]] * EXP2_SCALE - (new - bias[a][b]))
                for b in range(blocks)
            ]
            column = jnp.concatenate(parts, axis=0)
            totals.append(jnp.sum(column, axis=0, keepdims=True))
            columns.append(column.astype(jnp.bfloat16))
            news.append(new)
        new = jnp.concatenate(news, axis=1)
        fades[n] = jnp.exp2(m_sc[state] - new)
        m_sc[state] = new
        l_sc[state] = l_sc[state] * fades[n] + jnp.concatenate(totals, axis=1)
        weights[n] = jnp.concatenate(columns, axis=1)

    def mix(n):
        state, queries, keys, values, bias = tiles[n]
        mixed = jnp.dot(values, weights.pop(n), preferred_element_type=jnp.float32)
        acc_sc[state] = acc_sc[state] * fades.pop(n) + mixed

    score(0)
    for n in range(count):
        if n + 1 < count:
            score(n + 1)
        if n > 0:
            mix(n - 1)
        weigh(n)
    mix(count - 1)


def kernel(
    q_ref, k_ref, v_ref, qg_ref, kg_ref, adj_ref, frames_ref,
    out_ref,
    vs, ks, qs, adju, qn, kn, vt, stat, statr,
    bias_v, bias_s, m_sc, l_sc, acc_sc, obuf, rbuf, obuf4, rbuf4, ost, rst,
    ssem, bsem, rkv, rq, ra, rstat, ro, ro4, rost,
):
    z, h, k, t = place()
    other = 1 - k
    kv = (vs, ks)
    s_me = lax.axis_index("seq")
    upper = lax.div(h, 2)
    far_core = 1 - upper
    is_far = k == far_core

    def dev(zz, hh, kk):
        return (lax.rem(zz + PLANES, PLANES) * 8 + hh * 2 + kk, t)

    def chip(step):
        return lax.rem(h + step, CHIPS)

    sends = []

    def send(src, dst, rsem, device, condition=None):
        copy = pltpu.make_async_remote_copy(
            src_ref=src, dst_ref=dst, send_sem=ssem.at[len(sends)], recv_sem=rsem,
            device_id=device, device_id_type=MESH,
        )
        sends.append((copy, condition))
        if condition is None:
            copy.start()
        else:
            pl.when(condition)(copy.start)

    def send_kv(v, src, slot, device):
        send(src, kv[v].at[slot], rkv.at[v, slot], device)

    def arrived(dst, rsem):
        pltpu.make_async_copy(dst, dst, rsem).wait()

    def arrived_kv(v, slot):
        arrived(kv[v].at[slot], rkv.at[v, slot])

    barrier = pltpu.get_barrier_semaphore()
    peers = [dev(z, h, other)]
    for step in (1, 2, 3):
        peers += [dev(z, chip(step), 0), dev(z, chip(step), 1)]
    for zz in (z + 1, z - 1):
        peers += [dev(zz, h, 0), dev(zz, h, 1)]
    for step in range(1, TENSOR):
        peers.append((s_me, lax.rem(t + step, TENSOR)))
    for peer in peers:
        pl.semaphore_signal(barrier, inc=1, device_id=peer, device_id_type=MESH)

    eye = lax.broadcasted_iota(jnp.int32, (128, 128), 0) == lax.broadcasted_iota(
        jnp.int32, (128, 128), 1
    )
    rows = []
    for ref in (q_ref, k_ref):
        for half in range(2):
            part = ref[half * 128 : (half + 1) * 128, :]
            column = jnp.sum(part * part, axis=1, keepdims=True)
            rows.append(jnp.sum(jnp.where(eye, column, 0.0), axis=0, keepdims=True))
    mine = jnp.concatenate(rows + [jnp.zeros((4, 128), jnp.float32)], axis=0)
    stat[...] = mine
    statr[t] = mine

    def u_slot(position, core):
        return position + 12 - 4 * core

    own = 2 * h + k
    for i in range(HEADS):
        vt[i] = v_ref[:, i * HD : (i + 1) * HD].T
    vs[u_slot(own, k)] = vt[h]
    vs[COLUMN + 2 + k] = vt[4]
    m_sc[...] = jnp.full_like(m_sc, -1e29)
    l_sc[...] = jnp.zeros_like(l_sc)
    acc_sc[...] = jnp.zeros_like(acc_sc)

    pl.semaphore_wait(barrier, len(peers))

    for step in range(1, TENSOR):
        send(stat, statr.at[t], rstat.at[t], (s_me, lax.rem(t + step, TENSOR)))

    def spread_u(v, hp, src):
        p = 2 * hp + k
        send_kv(v, src, u_slot(p - 8, k), dev(z + 1, h, k))
        send_kv(v, src, u_slot(p + 8, k), dev(z - 1, h, k))
        send_kv(v, src, u_slot(p, other), dev(z, h, other))

    def first(v, ref):
        for step in (2, 1, 3):
            send_kv(v, ref.at[chip(step)], u_slot(own, k), dev(z, chip(step), k))
        spread_u(v, h, ref.at[h])
        send_kv(v, ref.at[4], COLUMN + k, dev(z + 1, h, k))
        send_kv(v, ref.at[4], COLUMN + 4 + k, dev(z - 1, h, k))
        send_kv(v, ref.at[4], COLUMN + 2 + k, dev(z, h, other))

    first(0, vt)

    core = upper
    place_q = 2 * lax.rem(h, 2) + k
    to_self = core == k
    to_other = jnp.logical_not(to_self)
    for step in (1, 2, 3):
        send(adj_ref, adju.at[place_q], ra.at[place_q], dev(z, chip(step), core))
    send(adj_ref, adju.at[place_q], ra.at[place_q], dev(z, h, other), to_other)

    for step in range(1, TENSOR):
        j = lax.rem(t + step, TENSOR)
        arrived(statr.at[j], rstat.at[j])
    total = statr[0]
    for j in range(1, TENSOR):
        total = total + statr[j]
    inverse = 1.0 / jnp.sqrt(total / float(HD * HEADS * TENSOR) + EPS)

    def normalize(row, half, ref, gain, put):
        lane_row = inverse[row + half : row + half + 1, :]
        column = jnp.sum(jnp.where(eye, lane_row, 0.0), axis=1, keepdims=True)
        span = slice(half * 128, (half + 1) * 128)
        for i in range(HEADS):
            feature = slice(i * HD, (i + 1) * HD)
            put(i, span, ref[span, feature] * column * gain[feature][None, :])

    def put_k(i, span, x):
        kn[i, span, :] = x.astype(jnp.bfloat16)

    def put_q(i, span, x):
        qn[i, :, span] = x.T.astype(jnp.bfloat16)

    normalize(2, 0, k_ref, kg_ref, put_k)
    normalize(2, 1, k_ref, kg_ref, put_k)
    normalize(0, 0, q_ref, qg_ref, put_q)
    first(1, kn)
    ks[u_slot(own, k)] = kn[h]
    ks[COLUMN + 2 + k] = kn[4]
    normalize(0, 1, q_ref, qg_ref, put_q)

    @pl.when(to_self)
    def _():
        qs[place_q] = qn[h]
        qs[4 + place_q] = qn[4]
        adju[place_q] = adj_ref[...]

    for base, head in ((0, chip), (4, lambda step: 4)):
        at = base + place_q
        for step in (2, 1, 3):
            send(qn.at[head(step)], qs.at[at], rq.at[at], dev(z, chip(step), core))
        send(qn.at[head(0)], qs.at[at], rq.at[at], dev(z, h, other), to_other)

    def plane_u(v, step):
        slot = u_slot(2 * chip(step) + k, k)
        arrived_kv(v, slot)
        spread_u(v, chip(step), kv[v].at[slot])

    def planes_u(v, step):
        hp = chip(step)
        sign = 1 - 2 * lax.div(hp, 2)
        p = 2 * hp + k
        for q in (p - 8, p + 8):
            arrived_kv(v, u_slot(q, k))
        far = lax.div(1 + sign, 2)
        send_kv(
            v, kv[v].at[u_slot(p + 8 * sign, k)], u_slot(p + 16 * sign, far),
            dev(z - sign, h, far),
        )
        for q in (p - 8, p + 8):
            send_kv(v, kv[v].at[u_slot(q, k)], u_slot(q, other), dev(z, h, other))

    def planes_4(v):
        low, high = COLUMN + k, COLUMN + 4 + k
        arrived_kv(v, low)
        arrived_kv(v, high)
        send_kv(
            v, kv[v].at[COLUMN + 4 * far_core + k], COLUMN + 6 + k,
            dev(z + 2 * upper - 1, h, far_core),
        )
        for slot in (low, high):
            send_kv(v, kv[v].at[slot], slot, dev(z, h, other))

    def mine_q(i):
        return jnp.logical_and(to_self, place_q == i)

    def unless_mine(i, wait):
        pl.when(jnp.logical_not(mine_q(i)))(wait)

    def biases_ready():
        frame_row = frames_ref[...][None, :]
        lane = lax.broadcasted_iota(jnp.int32, (1, 128), 1)
        rows = []
        for i in range(4):
            unless_mine(i, lambda: arrived(adju.at[i], ra.at[i]))
            shard = 8 * z + 4 * k + i
            for a in range(2):
                at = jnp.where(lane == 2 * shard + a, frame_row, -1)
                gap = jnp.abs(frame_row - jnp.max(at, axis=1, keepdims=True))
                fine = (gap == 0) | ((gap == 1) & (adju[i, a : a + 1, :] == 1))
                rows.append(jnp.where(fine, 0.0, BLOCKED))
        bias_v[...] = jnp.concatenate(rows, axis=0)

    def bias_copy():
        return pltpu.make_async_copy(bias_v, bias_s, bsem)

    def bias_of(i, first_shard):
        found = [[], []]
        for shard in (first_shard, first_shard + 1):
            valid = jnp.logical_and(shard >= 0, shard < 64)
            at = jnp.clip(shard, 0, 63)
            for a in range(2):
                for b in range(2):
                    found[a].append(jnp.where(valid, bias_s[2 * i + a, 2 * at + b], BLOCKED))
        return found

    def unit(n, carry):
        step = jnp.where(
            n < 3, 0, jnp.where(n < 5, 2 * n - 5, jnp.where(n < 7, 1, jnp.where(n < 9, 3, 2)))
        )
        turn = jnp.where(
            n < 3, n, jnp.where(n < 5, 0, jnp.where(n < 7, n - 4, jnp.where(n < 9, n - 6, n - 9)))
        )
        dz = jnp.where(turn == 0, 0, 2 * turn - 3)
        slot = jnp.where(
            n >= 12, 24 * k + 2 * (n - 12), u_slot(8 * dz + 2 * lax.rem(h + step, CHIPS), k)
        )
        shard = 8 * z + 4 * k + slot - 12
        turn4 = n - 14
        dz4 = jnp.where(turn4 == 3, 2 - 4 * upper, jnp.where(turn4 == 0, 0, 2 * turn4 - 3))
        slot4 = COLUMN + jnp.where(turn4 == 0, 2, jnp.where(turn4 == 1, 0, 2 * turn4))
        column = n >= 14
        slot = jnp.where(column, slot4, slot)
        shard = jnp.where(column, 8 * (z + dz4) + 2 * h, shard)
        base = jnp.where(column, 4, 0)
        keys = ks[pl.ds(slot, 2)].reshape(2 * TOK, HD)
        values = jnp.concatenate([vs[slot], vs[slot + 1]], axis=1)
        fold(
            [(base + i, qs[base + i], keys, values, bias_of(i, shard)) for i in range(4)],
            m_sc, l_sc, acc_sc,
        )
        return carry

    def from_partner(dz, step):
        for v in range(2):
            arrived_kv(v, u_slot(8 * dz + 2 * chip(step) + other, k))

    def compute(begin, end):
        lax.fori_loop(begin, end, unit, 0)

    planes_u(0, 0)
    planes_4(0)
    plane_u(0, 1)
    plane_u(0, 3)
    plane_u(0, 2)
    biases_ready()
    planes_u(1, 0)
    planes_4(1)
    planes_u(0, 1)
    planes_u(0, 3)
    plane_u(1, 1)
    plane_u(1, 3)
    bias_copy().start()
    planes_u(0, 2)
    plane_u(1, 2)
    planes_u(1, 1)
    planes_u(1, 3)
    bias_copy().wait()
    for i in range(4):
        unless_mine(i, lambda: arrived(qs.at[i], rq.at[i]))
    for dz in (0, -1, 1):
        from_partner(dz, 0)
    compute(0, 3)
    planes_u(1, 2)
    for step in (1, 3):
        from_partner(0, step)
        from_partner(-1, step)
        from_partner(1, step)
    compute(3, 9)

    for i in range(4):
        unless_mine(i, lambda: arrived(qs.at[4 + i], rq.at[4 + i]))
    for v in range(2):
        for slot in (0, 2, 4):
            arrived_kv(v, COLUMN + slot + other)

        @pl.when(is_far)
        def _():
            arrived_kv(v, COLUMN + 6)
            arrived_kv(v, COLUMN + 7)

    compute(14, jnp.where(is_far, 18, 17))
    for i in range(4):
        total = l_sc[4 + i]
        obuf4[i] = (acc_sc[4 + i] / jnp.maximum(total, 1e-30)).astype(jnp.bfloat16)
        ost[i] = jnp.concatenate([m_sc[4 + i], total], axis=0)

    def owner(i):
        return 2 * k + i // 2, i % 2

    def away(i):
        hh, kk = owner(i)
        return jnp.logical_not(jnp.logical_and(hh == h, kk == k))

    def give(i, src, dst, rsem):
        send(src.at[i], dst.at[h], rsem.at[h], dev(z, *owner(i)), away(i))

        @pl.when(jnp.logical_not(away(i)))
        def _():
            dst[h] = src[i]

    from_partner(0, 2)
    from_partner(-1, 2)
    from_partner(1, 2)
    for v in range(2):
        for i in range(4):
            arrived_kv(v, 24 * k + i)
    for i in range(4):
        give(i, obuf4, rbuf4, ro4)
        give(i, ost, rst, rost)
    compute(9, 14)

    for i in range(4):
        obuf[i] = (acc_sc[i] / l_sc[i]).T.astype(jnp.bfloat16)
        if i > 0:
            give(i - 1, obuf, rbuf, ro)

    def returned(head, dst, rsem):
        pl.when(jnp.logical_not(jnp.logical_and(to_self, head == h)))(
            lambda: arrived(dst.at[head], rsem.at[head])
        )

    for head in range(4):
        returned(head, rbuf4, ro4)
        returned(head, rst, rost)
    give(3, obuf, rbuf, ro)
    top = jnp.maximum(
        jnp.maximum(rst[0, 0:1], rst[1, 0:1]), jnp.maximum(rst[2, 0:1], rst[3, 0:1])
    )
    shares = [rst[j, 1:2] * jnp.exp2(rst[j, 0:1] - top) for j in range(4)]
    whole = shares[0] + shares[1] + shares[2] + shares[3]
    merged = rbuf4[0].astype(jnp.float32) * shares[0]
    for j in range(1, 4):
        merged = merged + rbuf4[j].astype(jnp.float32) * shares[j]
    out_ref[:, 4 * HD :] = (merged / whole).T
    for head in range(4):
        returned(head, rbuf, ro)
    for head in range(4):
        out_ref[:, head * HD : (head + 1) * HD] = rbuf[head].astype(jnp.float32)

    for copy, condition in sends:
        if condition is None:
            copy.wait_send()
        else:
            pl.when(condition)(copy.wait_send)


def shards(q_in, k_in, v_in, q_gain, k_gain, frames, adjacent):
    vmem = pl.BlockSpec(memory_space=pltpu.VMEM)
    bf16, f32, dma = jnp.bfloat16, jnp.float32, pltpu.SemaphoreType.DMA
    return pl.pallas_call(
        kernel,
        name="window_attention",
        out_shape=jax.ShapeDtypeStruct((TOK, HEADS * HD), f32),
        in_specs=[vmem] * 7,
        out_specs=vmem,
        scratch_shapes=[
            pltpu.VMEM((SLOTS, HD, TOK), bf16),
            pltpu.VMEM((SLOTS, TOK, HD), bf16),
            pltpu.VMEM((8, HD, TOK), bf16),
            pltpu.VMEM((4, 2, 128), jnp.int32),
            pltpu.VMEM((HEADS, HD, TOK), bf16),
            pltpu.VMEM((HEADS, TOK, HD), bf16),
            pltpu.VMEM((HEADS, HD, TOK), bf16),
            pltpu.VMEM((8, 128), f32),
            pltpu.VMEM((TENSOR, 8, 128), f32),
            pltpu.VMEM((8, 128), f32),
            pltpu.SMEM((8, 128), f32),
            pltpu.VMEM((8, 1, TOK), f32),
            pltpu.VMEM((8, 1, TOK), f32),
            pltpu.VMEM((8, HD, TOK), f32),
            pltpu.VMEM((4, TOK, HD), bf16),
            pltpu.VMEM((4, TOK, HD), bf16),
            pltpu.VMEM((4, HD, TOK), bf16),
            pltpu.VMEM((4, HD, TOK), bf16),
            pltpu.VMEM((4, 2, TOK), f32),
            pltpu.VMEM((4, 2, TOK), f32),
            dma((128,)),
            dma,
            dma((2, SLOTS)),
            dma((8,)),
            dma((4,)),
            dma((TENSOR,)),
            dma((4,)),
            dma((4,)),
            dma((4,)),
        ],
        compiler_params=pltpu.CompilerParams(collective_id=0, has_side_effects=True),
    )(q_in, k_in, v_in, q_gain, k_gain, adjacent, frames)


def solution(mesh):
    return jax.shard_map(
        shards,
        mesh=mesh,
        in_specs=(
            P("seq", "tensor"),
            P("seq", "tensor"),
            P("seq", "tensor"),
            P("tensor"),
            P("tensor"),
            P(),
            P("seq", None),
        ),
        out_specs=P("seq", "tensor"),
        check_vma=False,
    )
```

time: 85.1 us -> 77 us (0.905)
  the two profiles are of different devices: /device:TPU:1 before, /device:TPU:57 now
where the time goes in v4:
time: 77 us; the launch traced here: 76 us
  Pallas kernels  74 us (96%)
  local copies, waits for them, and re-layouts  1.97 us (3%)
    pallas_call x1, Pallas kernels, shards(): pl.pallas_call(kernel, name='window_attention', out_shape=jax.ShapeDtypeS...  74 us
    unnamed x1, local copies, waits for them, and re-layouts  1.97 us

profile of v4, /device:TPU:57, one launch (start us, length us, event | category | flops | bytes accessed | tf_op | source)
XLA Modules:
  0.0 76.0 jit_solution(5637874347909724201)
XLA Ops:
  0.0 74.0 %window_attention.1 = f32[256,640]{1,0:T(8,128)} custom-call(f32[256,640]{1,0:T(8,128)} %q_ref.1, f32[256,640]{1,0:T(8,128)} %k_ref.1, bf16[256,640]{1,0:T(8,128)(2,1)} %v_ref.1, f32[640]{0:T(1024)} %qg_ref.1, f32[640]{0:T(1024)} %kg_ref.1, s32[2,128]{1,0:T(2,128)} %adj_ref.1, s32[128]{0:T(128)} %frames_ref.1), custom_call_target="tpu_custom_call" | custom-call | tf_op jit(solution)/shard_map/window_attention/pallas_call | solution.py:434
  74.0 2.0 %copy.9 = f32[256,640]{1,0:T(8,128)} copy(f32[256,640]{1,0:T(8,128)} %window_attention.1) | data formatting | bytes 1310720

commit v5 on v4

--- a/solution.py
+++ b/solution.py
@@ -75,11 +75,12 @@
 
 
 def kernel(
-    q_ref, k_ref, v_ref, qg_ref, kg_ref, adj_ref, frames_ref,
+    q_hbm, k_hbm, v_hbm, qg_ref, kg_ref, adj_ref, frames_ref,
     out_ref,
+    q_ref, k_ref, v_ref,
     vs, ks, qs, adju, qn, kn, vt, stat, statr,
     bias_v, bias_s, m_sc, l_sc, acc_sc, obuf, rbuf, obuf4, rbuf4, ost, rst,
-    ssem, bsem, rkv, rq, ra, rstat, ro, ro4, rost,
+    ssem, bsem, isem, rkv, rq, ra, rstat, ro, ro4, rost,
 ):
     z, h, k, t = place()
     other = 1 - k
@@ -116,6 +117,13 @@
 
     def arrived_kv(v, slot):
         arrived(kv[v].at[slot], rkv.at[v, slot])
+
+    loads = [
+        pltpu.make_async_copy(src, dst, isem.at[n])
+        for n, (src, dst) in enumerate(((q_hbm, q_ref), (k_hbm, k_ref), (v_hbm, v_ref)))
+    ]
+    for load in loads:
+        load.start()
 
     barrier = pltpu.get_barrier_semaphore()
     peers = [dev(z, h, other)]
@@ -127,6 +135,9 @@
         peers.append((s_me, lax.rem(t + step, TENSOR)))
     for peer in peers:
         pl.semaphore_signal(barrier, inc=1, device_id=peer, device_id_type=MESH)
+
+    for load in loads:
+        load.wait()
 
     eye = lax.broadcasted_iota(jnp.int32, (128, 128), 0) == lax.broadcasted_iota(
         jnp.int32, (128, 128), 1
@@ -164,15 +175,18 @@
         send_kv(v, src, u_slot(p + 8, k), dev(z - 1, h, k))
         send_kv(v, src, u_slot(p, other), dev(z, h, other))
 
-    def first(v, ref):
-        for step in (2, 1, 3):
+    def first_y(v, ref, steps):
+        for step in steps:
             send_kv(v, ref.at[chip(step)], u_slot(own, k), dev(z, chip(step), k))
+
+    def first_z(v, ref):
         spread_u(v, h, ref.at[h])
         send_kv(v, ref.at[4], COLUMN + k, dev(z + 1, h, k))
         send_kv(v, ref.at[4], COLUMN + 4 + k, dev(z - 1, h, k))
         send_kv(v, ref.at[4], COLUMN + 2 + k, dev(z, h, other))
 
-    first(0, vt)
+    first_y(0, vt, (2, 1, 3))
+    first_z(0, vt)
 
     core = upper
     place_q = 2 * lax.rem(h, 2) + k
@@ -207,7 +221,7 @@
     normalize(2, 0, k_ref, kg_ref, put_k)
     normalize(2, 1, k_ref, kg_ref, put_k)
     normalize(0, 0, q_ref, qg_ref, put_q)
-    first(1, kn)
+    first_z(1, kn)
     ks[u_slot(own, k)] = kn[h]
     ks[COLUMN + 2 + k] = kn[4]
     normalize(0, 1, q_ref, qg_ref, put_q)
@@ -223,6 +237,7 @@
         for step in (2, 1, 3):
             send(qn.at[head(step)], qs.at[at], rq.at[at], dev(z, chip(step), core))
         send(qn.at[head(0)], qs.at[at], rq.at[at], dev(z, h, other), to_other)
+    first_y(1, kn, (1, 3, 2))
 
     def plane_u(v, step):
         slot = u_slot(2 * chip(step) + k, k)
@@ -287,7 +302,7 @@
                     found[a].append(jnp.where(valid, bias_s[2 * i + a, 2 * at + b], BLOCKED))
         return found
 
-    def unit(n, carry):
+    def keys_of(n):
         step = jnp.where(
             n < 3, 0, jnp.where(n < 5, 2 * n - 5, jnp.where(n < 7, 1, jnp.where(n < 9, 3, 2)))
         )
@@ -305,21 +320,50 @@
         column = n >= 14
         slot = jnp.where(column, slot4, slot)
         shard = jnp.where(column, 8 * (z + dz4) + 2 * h, shard)
-        base = jnp.where(column, 4, 0)
         keys = ks[pl.ds(slot, 2)].reshape(2 * TOK, HD)
         values = jnp.concatenate([vs[slot], vs[slot + 1]], axis=1)
+        return keys, values, shard, jnp.where(column, 4, 0)
+
+    def unit(n, carry):
+        keys, values, shard, base = keys_of(n)
         fold(
             [(base + i, qs[base + i], keys, values, bias_of(i, shard)) for i in range(4)],
             m_sc, l_sc, acc_sc,
         )
         return carry
 
+    def last_units(low):
+        def pair(j, carry):
+            tiles = []
+            for n in (10 + 2 * j, 11 + 2 * j):
+                keys, values, shard, _ = keys_of(n)
+                for i in (low, low + 1):
+                    tiles.append((i, qs[i], keys, values, bias_of(i, shard)))
+            fold(tiles, m_sc, l_sc, acc_sc)
+            return carry
+
+        lax.fori_loop(0, 2, pair, 0)
+
     def from_partner(dz, step):
         for v in range(2):
             arrived_kv(v, u_slot(8 * dz + 2 * chip(step) + other, k))
 
     def compute(begin, end):
         lax.fori_loop(begin, end, unit, 0)
+
+    def owner(i):
+        return 2 * k + i // 2, i % 2
+
+    def away(i):
+        hh, kk = owner(i)
+        return jnp.logical_not(jnp.logical_and(hh == h, kk == k))
+
+    def give(i, src, dst, rsem):
+        send(src.at[i], dst.at[h], rsem.at[h], dev(z, *owner(i)), away(i))
+
+        @pl.when(jnp.logical_not(away(i)))
+        def _():
+            dst[h] = src[i]
 
     planes_u(0, 0)
     planes_4(0)
@@ -331,25 +375,14 @@
     planes_4(1)
     planes_u(0, 1)
     planes_u(0, 3)
-    plane_u(1, 1)
-    plane_u(1, 3)
     bias_copy().start()
     planes_u(0, 2)
-    plane_u(1, 2)
-    planes_u(1, 1)
-    planes_u(1, 3)
     bias_copy().wait()
     for i in range(4):
         unless_mine(i, lambda: arrived(qs.at[i], rq.at[i]))
     for dz in (0, -1, 1):
         from_partner(dz, 0)
     compute(0, 3)
-    planes_u(1, 2)
-    for step in (1, 3):
-        from_partner(0, step)
-        from_partner(-1, step)
-        from_partner(1, step)
-    compute(3, 9)
 
     for i in range(4):
         unless_mine(i, lambda: arrived(qs.at[4 + i], rq.at[4 + i]))
@@ -362,41 +395,42 @@
             arrived_kv(v, COLUMN + 6)
             arrived_kv(v, COLUMN + 7)
 
-    compute(14, jnp.where(is_far, 18, 17))
+    compute(14, 16)
+    plane_u(1, 1)
+    plane_u(1, 3)
+    compute(16, jnp.where(is_far, 18, 17))
     for i in range(4):
         total = l_sc[4 + i]
         obuf4[i] = (acc_sc[4 + i] / jnp.maximum(total, 1e-30)).astype(jnp.bfloat16)
         ost[i] = jnp.concatenate([m_sc[4 + i], total], axis=0)
-
-    def owner(i):
-        return 2 * k + i // 2, i % 2
-
-    def away(i):
-        hh, kk = owner(i)
-        return jnp.logical_not(jnp.logical_and(hh == h, kk == k))
-
-    def give(i, src, dst, rsem):
-        send(src.at[i], dst.at[h], rsem.at[h], dev(z, *owner(i)), away(i))
-
-        @pl.when(jnp.logical_not(away(i)))
-        def _():
-            dst[h] = src[i]
-
+    plane_u(1, 2)
+    for i in range(4):
+        give(i, obuf4, rbuf4, ro4)
+        give(i, ost, rst, rost)
+    planes_u(1, 1)
+    planes_u(1, 3)
+    for step in (1, 3):
+        from_partner(0, step)
+    compute(3, 5)
+    planes_u(1, 2)
+    for step in (1, 3):
+        from_partner(-1, step)
+        from_partner(1, step)
+    compute(5, 9)
     from_partner(0, 2)
     from_partner(-1, 2)
     from_partner(1, 2)
     for v in range(2):
         for i in range(4):
             arrived_kv(v, 24 * k + i)
-    for i in range(4):
-        give(i, obuf4, rbuf4, ro4)
-        give(i, ost, rst, rost)
-    compute(9, 14)
-
-    for i in range(4):
-        obuf[i] = (acc_sc[i] / l_sc[i]).T.astype(jnp.bfloat16)
-        if i > 0:
-            give(i - 1, obuf, rbuf, ro)
+    compute(9, 10)
+
+    for low in (0, 2):
+        last_units(low)
+        for i in (low, low + 1):
+            obuf[i] = (acc_sc[i] / l_sc[i]).T.astype(jnp.bfloat16)
+        for i in (low, low + 1):
+            give(i, obuf, rbuf, ro)
 
     def returned(head, dst, rsem):
         pl.when(jnp.logical_not(jnp.logical_and(to_self, head == h)))(
@@ -406,7 +440,6 @@
     for head in range(4):
         returned(head, rbuf4, ro4)
         returned(head, rst, rost)
-    give(3, obuf, rbuf, ro)
     top = jnp.maximum(
         jnp.maximum(rst[0, 0:1], rst[1, 0:1]), jnp.maximum(rst[2, 0:1], rst[3, 0:1])
     )
@@ -435,9 +468,12 @@
         kernel,
         name="window_attention",
         out_shape=jax.ShapeDtypeStruct((TOK, HEADS * HD), f32),
-        in_specs=[vmem] * 7,
+        in_specs=[pl.BlockSpec(memory_space=pl.ANY)] * 3 + [vmem] * 4,
         out_specs=vmem,
         scratch_shapes=[
+            pltpu.VMEM((TOK, HEADS * HD), f32),
+            pltpu.VMEM((TOK, HEADS * HD), f32),
+            pltpu.VMEM((TOK, HEADS * HD), bf16),
             pltpu.VMEM((SLOTS, HD, TOK), bf16),
             pltpu.VMEM((SLOTS, TOK, HD), bf16),
             pltpu.VMEM((8, HD, TOK), bf16),
@@ -460,6 +496,7 @@
             pltpu.VMEM((4, 2, TOK), f32),
             dma((128,)),
             dma,
+            dma((3,)),
             dma((2, SLOTS)),
             dma((8,)),
             dma((4,)),

time: 77 us -> 71.3 us (0.926); the launches traced: 76 us -> 71.1 us
  Pallas kernels: 74 us -> 69.1 us
    pallas_call x1, Pallas kernels: 74 us -> 69.1 us  [shards(): pl.pallas_call(kernel, name='window_attention', out_shape=jax.ShapeDtypeS...]
where the time goes in v5:
time: 71.3 us; the launch traced here: 71.1 us
  Pallas kernels  69.1 us (97%)
  local copies, waits for them, and re-layouts  1.97 us (3%)
    pallas_call x1, Pallas kernels, shards(): pl.pallas_call(kernel, name='window_attention', out_shape=jax.ShapeDtypeS...  69.1 us
    unnamed x1, local copies, waits for them, and re-layouts  1.97 us

profile of v5, /device:TPU:57, one launch (start us, length us, event | category | flops | bytes accessed | tf_op | source)
XLA Modules:
  0.0 71.1 jit_solution(3492199502533006966)
XLA Ops:
  0.0 69.1 %window_attention.1 = f32[256,640]{1,0:T(8,128)} custom-call(f32[256,640]{1,0:T(8,128)} %q_hbm.1, f32[256,640]{1,0:T(8,128)} %k_hbm.1, bf16[256,640]{1,0:T(8,128)(2,1)} %v_hbm.1, f32[640]{0:T(1024)} %qg_ref.1, f32[640]{0:T(1024)} %kg_ref.1, s32[2,128]{1,0:T(2,128)} %adj_ref.1, s32[128]{0:T(128)} %frames_ref.1), custom_call_target="tpu_custom_call" | custom-call | tf_op jit(solution)/shard_map/window_attention/pallas_call | solution.py:467
  69.2 2.0 %copy.9 = f32[256,640]{1,0:T(8,128)} copy(f32[256,640]{1,0:T(8,128)} %window_attention.1) | data formatting | bytes 1310720
